TPU v7x, 128 devices: a whole 4x4x4 slice. The times are simulated.
128 devices in a mesh: row: 16 (over x, z_lo, core), col: 8 (over y, z_hi).
Axes of the slice: x: 4, y: 4, z: 4 (z_hi: 2, z_lo: 2; z = z_hi * 2 + z_lo), core: 2. Of those that a mesh axis runs over, the one named last changes fastest.
Arguments:
- phi: bfloat16 [80, 80, 80, 256], P('col', 'row'), may hold values from -1 to 1
- psi: bfloat16 [80, 80, 80, 256], P('col', 'row'), may hold values from -1 to 1
- points: int32 [16384], P(('row', 'col')), may hold values from 0 to 511999, as said below
Outputs:
- schur: float32 [16384, 16384], P('row', 'col')
- panel: float32 [16384, 256], P('row')
- potential: float32 [80, 80, 80, 256], P('col', 'row')
Inputs may be any that keep to these rules, and one draw needn't show every extreme that they name: `points`: block k of 128 consecutive entries holds distinct indices (x 80 + y) * 80 + z of cells with x // 10 = k mod (8) and y // 5 = k div (8).
All inputs are finite; a program needn't handle non-finite values.
Results may differ from a plain program's by a relative error of at most 0.0003.
Values may be sent and summed in bfloat16 or wider, within the bound.
A program may use at most 128 MiB of HBM per device.

v0:
```python
import math

import jax
import jax.numpy as jnp
from jax import lax
from jax.sharding import PartitionSpec as P

NMU = 16384
PB = 256
GX = 80
GY = 80
GZ = 80


shift_value = 4.0
box_length = 2.0
highest = lax.Precision.HIGHEST


def signed_of(index, length):
    return jnp.where(2 * index < length, index, index - length).astype(jnp.float32)


def signed_frequency(count, offset, length):
    index = offset + jnp.arange(count, dtype=jnp.int32)
    return signed_of(index, length)


def coulomb_table(x_freq, y_freq, z_freq):
    squared = x_freq[:, None, None] ** 2 + y_freq[None, :, None] ** 2 + z_freq[None, None, :] ** 2
    safe = jnp.maximum(squared, 1.0)
    return jnp.where(squared > 0.5, box_length * box_length / math.pi / safe, 0.0)


def twiddles(length):
    rows_iota = lax.broadcasted_iota(jnp.int32, (length, length), 0)
    cols_iota = lax.broadcasted_iota(jnp.int32, (length, length), 1)
    angle = (rows_iota * cols_iota % length).astype(jnp.float32) * (2.0 * math.pi / length)
    return (jnp.cos(angle), jnp.sin(angle))


def transform(stacked, form, length, inverse):
    cosine, sine = twiddles(length)
    real_part = stacked[0]
    imag_part = stacked[1]
    cos_real = jnp.einsum(form, cosine, real_part, precision=highest)
    cos_imag = jnp.einsum(form, cosine, imag_part, precision=highest)
    sin_real = jnp.einsum(form, sine, real_part, precision=highest)
    sin_imag = jnp.einsum(form, sine, imag_part, precision=highest)
    if inverse:
        factor = 1.0 / length
        return jnp.stack([(cos_real - sin_imag) * factor, (cos_imag + sin_real) * factor])
    return jnp.stack([cos_real + sin_imag, cos_imag - sin_real])


def hadamard_gram(left, right, left_index, right_index):
    first = jnp.dot(left[0], right[0].T, preferred_element_type=jnp.float32)
    second = jnp.dot(left[1], right[1].T, preferred_element_type=jnp.float32)
    return first * second + shift_value * (left_index[:, None] == right_index[None, :]).astype(
        jnp.float32
    )


def on_device(phi, psi, points):
    col_count = lax.axis_size("col")
    row_count = lax.axis_size("row")
    col_index = lax.axis_index("col")
    row_index = lax.axis_index("row")
    plane_count, line_count, depth_count, orbital_count = phi.shape
    cells = plane_count * line_count * depth_count
    flat_phi = phi.reshape(cells, orbital_count)
    flat_psi = psi.reshape(cells, orbital_count)
    global_x = points // (GY * GZ)
    global_y = points // GZ % GY
    global_z = points % GZ
    local_cell = (
        (global_x - col_index * plane_count) * line_count + global_y - row_index * line_count
    ) * GZ + global_z
    own_samples = jnp.stack(
        [jnp.take(flat_phi, local_cell, axis=0), jnp.take(flat_psi, local_cell, axis=0)]
    )
    row_block = NMU // row_count
    col_block = NMU // col_count
    every_sample = lax.all_gather(own_samples, ("row", "col"), axis=1, tiled=True)
    row_samples = lax.dynamic_slice_in_dim(every_sample, row_index * row_block, row_block, 1)
    col_samples = lax.dynamic_slice_in_dim(every_sample, col_index * col_block, col_block, 1)
    pivot = every_sample[:, :PB]
    row_global = row_index * row_block + jnp.arange(row_block, dtype=jnp.int32)
    col_global = col_index * col_block + jnp.arange(col_block, dtype=jnp.int32)
    pivots = jnp.arange(PB, dtype=jnp.int32)
    corner = hadamard_gram(pivot, pivot, pivots, pivots)
    lower_factor = jnp.linalg.cholesky(corner)
    inverse = lax.linalg.triangular_solve(
        lower_factor, jnp.eye(PB, dtype=jnp.float32), left_side=True, lower=True
    )
    pair_rows = jnp.dot(flat_phi, pivot[0].T, preferred_element_type=jnp.float32) * jnp.dot(
        flat_psi, pivot[1].T, preferred_element_type=jnp.float32
    )
    fitting = jnp.dot(pair_rows, inverse.T, precision=highest).reshape(
        plane_count, line_count, depth_count, PB
    )
    half_count = PB // 2
    packed = jnp.stack([fitting[..., :half_count], fitting[..., half_count:]])
    spectra = transform(packed, "kj,abjh->abkh", depth_count, False)
    spectra = transform(
        lax.all_to_all(spectra, "row", split_axis=3, concat_axis=2, tiled=True),
        "kj,ajch->akch",
        GY,
        False,
    )
    y_cells = GY // col_count
    z_cells = spectra.shape[3]
    kernel = coulomb_table(
        signed_frequency(GX, 0, GX),
        signed_frequency(y_cells, col_index * y_cells, GY),
        signed_frequency(z_cells, row_index * z_cells, GZ),
    )
    moved = transform(
        lax.all_to_all(spectra, "col", split_axis=2, concat_axis=1, tiled=True),
        "kj,jbch->kbch",
        GX,
        False,
    )
    spectra = transform(moved * kernel[None, :, :, :, None], "kj,jbch->kbch", GX, True)
    spectra = transform(
        lax.all_to_all(spectra, "col", split_axis=1, concat_axis=2, tiled=True),
        "kj,ajch->akch",
        GY,
        True,
    )
    spectra = transform(
        lax.all_to_all(spectra, "row", split_axis=2, concat_axis=3, tiled=True),
        "kj,abjh->abkh",
        GZ,
        True,
    )
    potential = jnp.concatenate([spectra[0], spectra[1]], axis=3)
    panel_rows = jnp.dot(
        hadamard_gram(row_samples, pivot, row_global, pivots), inverse.T, precision=highest
    )
    panel_cols = jnp.dot(
        hadamard_gram(col_samples, pivot, col_global, pivots), inverse.T, precision=highest
    )
    schur = hadamard_gram(row_samples, col_samples, row_global, col_global) - jnp.dot(
        panel_rows, panel_cols.T, precision=highest
    )
    return (schur, panel_rows, potential)


def solution(mesh):
    in_specs = (P("col", "row", None, None), P("col", "row", None, None), P(("row", "col")))
    out_specs = (P("row", "col"), P("row", None), P("col", "row", None, None))
    return jax.shard_map(
        on_device, mesh=mesh, in_specs=in_specs, out_specs=out_specs, check_vma=False
    )
```

profile of v0, /device:TPU:1, one launch (start us, length us, event | category | flops | bytes accessed | tf_op | source)
XLA Modules:
  0.0 813.3 jit_solution(13071163870392192607)
XLA Ops:
  13.1 326.4 %all-gather.2.cloned.1.call-done = bf16[2,16384,256]{2,1,0:T(8,128)(2,1)} async-done(((bf16[2,128,256]{2,1,0:T(8,128)(2,1)}), bf16[2,16384,256]{2,1,0:T(8,128)(2,1)}) %all-gather.2.cloned.1.call-update) | async-done | bytes 16777232 | tf_op jit(solution)/shard_map/all_gather | solution.py:84
  342.1 11.7 %cholesky.49 = f32[128,128]{1,0:T(8,128)S(1)} custom-call(f32[128,128]{1,0:T(8,128)S(1)} %cholesky.115), custom_call_target="Cholesky" | custom-call | tf_op jit(solution)/shard_map/jit(cholesky)/cholesky | solution.py:92
  353.9 9.8 %custom-call.14 = f32[1,128,128]{1,2,0:T(8,128)S(1)} custom-call(f32[1,128,128]{2,1,0:T(8,128)S(1)} %get-tuple-element.35), custom_call_target="InvertDiagBlocksLowerTriangular" | custom-call | tf_op jit(solution)/shard_map/jit(cholesky)/cholesky | solution.py:92
  364.2 11.7 %cholesky.103 = f32[128,128]{1,0:T(8,128)S(1)} custom-call(f32[128,128]{1,0:T(8,128)S(1)} %convolution_subtract_fusion.1), custom_call_target="Cholesky" | custom-call | tf_op jit(solution)/shard_map/jit(cholesky)/cholesky | solution.py:92
  378.0 4.0 while.1
  382.0 19.9 %custom-call.15 = f32[2,128,128]{1,2,0:T(8,128)S(1)} custom-call(f32[2,128,128]{2,1,0:T(8,128)S(1)} %get-tuple-element.11), custom_call_target="InvertDiagBlocksLowerTriangular" | custom-call | tf_op jit(solution)/shard_map/triangular_solve | solution.py:93
  416.3 12.5 %add_bitcast_fusion.2 = f32[1,10,5,80,128]{4,3,2,1,0:T(8,128)S(1)} fusion(f32[10,5,128,80]{2,3,1,0:T(8,128)S(1)} %fusion.7, f32[10,5,80,256]{3,2,1,0:T(8,128)S(1)} %bitcast.217), kind=kOutput, calls=%fused_computation.28 | convolution fusion | flops 492089600 | bytes 6144000 | tf_op jit(solution)/shard_map/kj,abjh->abkh/dot_general | solution.py:46
  432.3 52.9 %all_to_all.60 = f32[2,10,5,80,128]{4,0,2,1,3:T(2,128)S(1)} all-to-all(f32[2,10,5,80,128]{4,0,2,1,3:T(2,128)S(1)} %copy.46), channel_id=1, replica_groups=mesh['row'=16,'col'=8] {'row'}, dimensions={3} | all-to-all | bytes 8192000 | tf_op jit(solution)/shard_map/all_to_all | solution.py:106
  487.5 4.5 fusion.260
  503.1 4.3 squeeze.66
  515.9 5.1 copy.50
  521.0 6.5 all-to-all-start.1
  527.7 57.4 %all-to-all-done.1 = f32[2,10,80,5,128]{4,0,3,1,2:T(2,128)} async-done(((f32[2,10,80,5,128]{4,0,3,1,2:T(2,128)}), f32[2,10,80,5,128]{4,0,3,1,2:T(2,128)}, u32[]{:S(2)}, u32[]{:S(2)}) %all-to-all-start.1) | async-done | bytes 4096032 | tf_op jit(solution)/shard_map/all_to_all | solution.py:119
  585.1 3.9 copy.51
  589.0 4.5 fusion.259
  628.7 52.0 %all_to_all.61 = f32[2,80,10,5,128]{4,0,3,2,1:T(2,128)S(1)} all-to-all(f32[2,80,10,5,128]{4,0,3,2,1:T(2,128)S(1)} %copy.54), channel_id=1, replica_groups=mesh['row'=16,'col'=8] {'col'}, dimensions={1} | all-to-all | bytes 8192000 | tf_op jit(solution)/shard_map/all_to_all | solution.py:126
  680.7 4.5 fusion.258
  695.5 4.0 squeeze.72
  708.1 5.1 copy.57
  713.3 7.9 all-to-all-start.3
  736.3 10.3 %add_subtract_fusion = f32[1024,2048]{1,0:T(8,128)} fusion(f32[1024,2048]{1,0:T(8,128)S(1)} %fusion.19, f32[1024,2048]{1,0:T(8,128)S(1)} %fusion.20, f32[1024,256]{1,0:T(8,128)S(1)} %fusion.24, f32[2048,256]{1,0:T(8,128)S(1)} %fusion.23, s32[2048]{0:T(1024)S(1)} %iota_add_fusion, s32[1024]{0:T(1024)S(1)} %iota_add_fusion.1), kind=kOutput, calls=%fused_computation.4 | convolution fusion | flops 6452936704 | bytes 28323840 | tf_op jit(solution)/shard_map/dot_general | solution.py:144
  746.6 25.9 %all-to-all-done.3 = f32[2,10,80,5,128]{4,0,3,1,2:T(2,128)} async-done(((f32[2,10,80,5,128]{4,0,3,1,2:T(2,128)}), f32[2,10,80,5,128]{4,0,3,1,2:T(2,128)}, u32[]{:S(2)}, u32[]{:S(2)}) %all-to-all-start.3) | async-done | bytes 4096032 | tf_op jit(solution)/shard_map/all_to_all | solution.py:132
  776.4 4.5 fusion.257
  791.2 4.2 squeeze.74
  (129 shorter events, 147.2 us)
Async XLA Ops:
  7.2 1.6 copy-start
  7.2 332.3 %all-gather.2.cloned.1.call-start = ((), (), s32[]{:S(2)}) async-start(), calls=%async_computation.4 | async-start | bytes 16908288 | tf_op jit(solution)/shard_map/all_gather | solution.py:84
  402.8 1.8 copy-start.15
  497.1 3.4 copy-start.10
  507.4 3.8 copy-start.2
  507.4 3.8 copy-start.6
  521.0 64.1 %all-to-all-start.1 = ((f32[2,10,80,5,128]{4,0,3,1,2:T(2,128)}), f32[2,10,80,5,128]{4,0,3,1,2:T(2,128)}, u32[]{:S(2)}, u32[]{:S(2)}) async-start(f32[2,10,80,5,128]{4,0,3,1,2:T(2,128)} %copy.50), calls=%async_computation.1 | async-start | bytes 8192000 | tf_op jit(solution)/shard_map/all_to_all | solution.py:119
  598.6 3.3 copy-start.11
  608.2 3.7 copy-start.3
  608.2 3.7 copy-start.7
  689.9 3.4 copy-start.12
  699.5 3.8 copy-start.4
  699.5 3.8 copy-start.8
  713.3 59.2 %all-to-all-start.3 = ((f32[2,10,80,5,128]{4,0,3,1,2:T(2,128)}), f32[2,10,80,5,128]{4,0,3,1,2:T(2,128)}, u32[]{:S(2)}, u32[]{:S(2)}) async-start(f32[2,10,80,5,128]{4,0,3,1,2:T(2,128)} %copy.57), calls=%async_computation.3 | async-start | bytes 8192000 | tf_op jit(solution)/shard_map/all_to_all | solution.py:132
  725.1 11.2 %copy-start.14 = (f32[1024,256]{1,0:T(8,128)}, f32[1024,256]{1,0:T(8,128)S(1)}, u32[]{:S(2)}) copy-start(f32[1024,256]{1,0:T(8,128)S(1)} %fusion.24) | copy-start | bytes 3145732
  785.6 3.4 copy-start.13
  795.4 3.8 copy-start.5
  795.4 3.8 copy-start.9
  803.7 2.3 copy-start.1
Sparse Core Ops, SparseCore 0:
  13.1 326.3 all-gather.1
where the time goes:
time: 828 us; the launch traced here: 813 us
  waiting for transfers between devices  410 us (50%)
  matrix products  109 us (13%)
  blocking collectives  105 us (13%)
  local copies, waits for them, and re-layouts  98.3 us (12%)
  other arithmetic  60.2 us (7%)
  between operations  16.6 us (2%)
  starting transfers between devices  14.5 us (2%)
    all_gather x1, waiting for transfers between devices, on_device(): lax.all_gather(own_samples, ('row', 'col'), axis=1, tiled=True)  326 us
    all_to_all x1, waiting for transfers between devices, on_device(): lax.all_to_all(spectra, 'col', split_axis=2, concat_axis=1, tiled=True)  57.4 us
    all_to_all x1, blocking collectives, on_device(): lax.all_to_all(spectra, 'row', split_axis=3, concat_axis=2, tiled=True)  52.9 us
    all_to_all x1, blocking collectives, on_device(): lax.all_to_all(spectra, 'col', split_axis=1, concat_axis=2, tiled=True)  52 us
    another operation x6, other arithmetic, on_device(): lower_factor = jnp.linalg.cholesky(corner)  33.9 us
    dot_general x6, matrix products, transform(): cos_real = jnp.einsum(form, cosine, real_part, precision=highest)  29.7 us
    slice x8, local copies, waits for them, and re-layouts, transform(): real_part = stacked[0]  27 us
    all_to_all x1, waiting for transfers between devices, on_device(): lax.all_to_all(spectra, 'row', split_axis=2, concat_axis=3, tiled=True)  25.9 us
  transfers between devices with their start and end apart: 3, of which 3 were waited for; matrix products, arithmetic and copies ran while one was open for 3% of the time, Pallas kernels for 0%

commit v1 on v0

v1 whole, which is shorter than its diff:
```python
import functools
import math

import jax
import jax.numpy as jnp
import numpy as np
from jax import lax
from jax.experimental import pallas as pl
from jax.experimental.pallas import tpu as pltpu
from jax.sharding import PartitionSpec as P

NMU = 16384
PB = 256
N = 80
ROWS = 16
COLS = 8
CELLS = 4000
WIDE = 4096
CODE_LANE = 4000 - 31 * 128
LEVELS = 32766.0
LN2 = math.log(2.0)
shift_value = 4.0
highest = lax.Precision.HIGHEST
MESH = pl.DeviceIdType.MESH
VMEM = pl.BlockSpec(memory_space=pltpu.VMEM)
f32 = jnp.float32
bf16 = jnp.bfloat16


def hartley():
    angle = (np.outer(np.arange(N), np.arange(N)) % N) * (2.0 * np.pi / N)
    return np.cos(angle) + np.sin(angle)


def split_np(a):
    high = a.astype(np.float32).astype(jnp.bfloat16)
    low = (a - high.astype(np.float64)).astype(np.float32).astype(jnp.bfloat16)
    return high, low


def split(a):
    high = a.astype(bf16)
    return high, (a - high.astype(f32)).astype(bf16)


def mm(a, b):
    return jnp.dot(a, b, preferred_element_type=f32)


def mm_nt(a, b):
    return lax.dot_general(a, b, (((1,), (1,)), ((), ())), preferred_element_type=f32)


def scale_of(code):
    return jnp.exp(code.astype(f32) * (LN2 / 256.0))


def encode(peak):
    code = jnp.ceil(jnp.log(jnp.maximum(peak, 1e-30)) * (256.0 / LN2))
    return code, jnp.exp(code * (LN2 / 256.0))


def quantize(values, factor):
    q = jnp.clip(jnp.round(values * factor), -32767.0, 32767.0)
    return q.astype(jnp.int32).astype(jnp.int16)


def store_codes(out_ref, source_ref, peak):
    code, scale = encode(peak)
    factor = LEVELS / scale

    @pl.loop(0, 7)
    def _(j):
        at = pl.ds(pl.multiple_of(j * 512, 512), 512)
        out_ref[:, at] = quantize(source_ref[:, at], factor)

    out_ref[:, 3584:3968] = quantize(source_ref[:, 3584:3968], factor)
    last = jnp.clip(jnp.round(source_ref[:, 3968:4096] * factor), -32767.0, 32767.0)
    lane = lax.broadcasted_iota(jnp.int32, last.shape, 1)
    last = jnp.where(lane < CODE_LANE, last, jnp.where(lane == CODE_LANE, code, 0.0))
    out_ref[:, 3968:4096] = last.astype(jnp.int32).astype(jnp.int16)


def pivot_kernel(own_ref, out_ref, send1, recv1, send2, recv2, send3, recv3, local):
    r = lax.axis_index("row")
    c = lax.axis_index("col")
    barrier = pltpu.get_barrier_semaphore()
    for d in range(1, COLS):
        pl.semaphore_signal(
            barrier, inc=1, device_id={"row": r, "col": lax.rem(c + d, COLS)}, device_id_type=MESH
        )
    for d in range(1, ROWS):
        pl.semaphore_signal(
            barrier, inc=1, device_id={"row": lax.rem(r + d, ROWS), "col": c}, device_id_type=MESH
        )
    pl.semaphore_wait(barrier, COLS + ROWS - 2)

    def scatter(owner, j):
        return pltpu.make_async_remote_copy(
            own_ref.at[pl.ds(pl.multiple_of(j * 16, 16), 16)],
            out_ref.at[j, owner],
            send1.at[j],
            recv1.at[owner],
            device_id={"row": 0, "col": j},
            device_id_type=MESH,
        )

    for owner in range(2):

        @pl.when((r == 0) & (c == owner))
        def _():
            keep = pltpu.make_async_copy(
                own_ref.at[pl.ds(owner * 16, 16)], out_ref.at[owner, owner], local
            )
            keep.start()
            for d in range(1, COLS):
                scatter(owner, (owner + d) % COLS).start()
            keep.wait()

        @pl.when((r == 0) & (c != owner))
        def _():
            scatter(owner, c).wait_recv()

    def down(d):
        return pltpu.make_async_remote_copy(
            out_ref.at[c],
            out_ref.at[c],
            send2.at[d],
            recv2,
            device_id={"row": d, "col": c},
            device_id_type=MESH,
        )

    @pl.when(r == 0)
    def _():
        for d in range(1, ROWS):
            down(d).start()

    @pl.when(r != 0)
    def _():
        down(1).wait_recv()

    def across(d):
        return pltpu.make_async_remote_copy(
            out_ref.at[c],
            out_ref.at[c],
            send3.at[d],
            recv3.at[d],
            device_id={"row": r, "col": lax.rem(c + d, COLS)},
            device_id_type=MESH,
        )

    for d in range(1, COLS):
        across(d).start()
    for d in range(1, COLS):
        source = lax.rem(c + COLS - d, COLS)
        pltpu.make_async_remote_copy(
            out_ref.at[source],
            out_ref.at[source],
            send3.at[d],
            recv3.at[d],
            device_id={"row": r, "col": source},
            device_id_type=MESH,
        ).wait_recv()
    for d in range(1, COLS):
        across(d).wait_send()

    @pl.when(r == 0)
    def _():
        for d in range(1, ROWS):
            down(d).wait_send()

    for owner in range(2):

        @pl.when((r == 0) & (c == owner))
        def _():
            for d in range(1, COLS):
                scatter(owner, (owner + d) % COLS).wait_send()


def pivots_everywhere(own):
    dma = pltpu.SemaphoreType.DMA
    return pl.pallas_call(
        pivot_kernel,
        out_shape=jax.ShapeDtypeStruct((COLS, 2, 16, 2 * PB), bf16),
        in_specs=[VMEM],
        out_specs=VMEM,
        scratch_shapes=[
            dma((COLS,)),
            dma((2,)),
            dma((ROWS,)),
            dma,
            dma((COLS,)),
            dma((COLS,)),
            dma,
        ],
        compiler_params=pltpu.CompilerParams(collective_id=1, has_side_effects=True),
        name="pivots",
    )(own)


def pivot_halves(pivot_ref):
    rows = [pivot_ref[:, owner].reshape(128, 2 * PB) for owner in range(2)]
    both = jnp.concatenate(rows, axis=0)
    return both[:, :PB], both[:, PB:]


def cholesky_kernel(pivot_ref, inv_ref, w):
    pa, pb = pivot_halves(pivot_ref)
    i0 = lax.broadcasted_iota(jnp.int32, (PB, PB), 0)
    i1 = lax.broadcasted_iota(jnp.int32, (PB, PB), 1)
    eye = (i0 == i1).astype(f32)
    w[:, :PB] = mm_nt(pa, pa) * mm_nt(pb, pb) + shift_value * eye
    w[:, PB:] = eye
    nb = 32
    for block in range(PB // nb):
        g = block * nb
        panel = w[g : g + nb, :]
        sub = lax.broadcasted_iota(jnp.int32, (nb, 128), 0)
        for j in range(0, nb, 8):
            cols = [
                jnp.broadcast_to(panel[:, g + j + t : g + j + t + 1], (nb, 128)) for t in range(8)
            ]
            for t in range(8):
                k = j + t
                pivot = jnp.broadcast_to(cols[t][k : k + 1, :], (nb, 128))
                root = lax.rsqrt(pivot)
                root = root * (1.5 - 0.5 * pivot * root * root)
                left = cols[t] * root
                for u in range(t + 1, 8):
                    cols[u] = cols[u] - left * jnp.broadcast_to(
                        left[j + u : j + u + 1, :], (nb, 128)
                    )
                below = jnp.where(sub > k, left, 0.0)
                below = jnp.where(sub == k, 1.0 - root, below)
                wide = jnp.concatenate([below] * 4, axis=1)
                line = jnp.broadcast_to(panel[k : k + 1, :], (nb, 2 * PB))
                scaled = line * jnp.concatenate([root] * 4, axis=1)
                row_k = jnp.concatenate([sub == k] * 4, axis=1)
                panel = jnp.where(row_k, scaled, panel - wide * scaled)
        w[g : g + nb, :] = panel
        if g + nb < PB:
            left = panel[:, g + nb : PB] if (g + nb) % 128 == 0 else panel[:, :PB]
            if (g + nb) % 128 == 0:
                update = lax.dot_general(
                    left, panel, (((0,), (0,)), ((), ())), precision=highest, preferred_element_type=f32
                )
                w[g + nb :, :] = w[g + nb :, :] - update
            else:
                update = lax.dot_general(
                    left, panel, (((0,), (0,)), ((), ())), precision=highest, preferred_element_type=f32
                )
                w[g + nb :, :] = w[g + nb :, :] - update[g + nb :, :]
    inv_ref[...] = jnp.where(i0 >= i1, w[:, PB:], 0.0)


def inverse_factor(pivots):
    return pl.pallas_call(
        cholesky_kernel,
        out_shape=jax.ShapeDtypeStruct((PB, PB), f32),
        in_specs=[VMEM],
        out_specs=VMEM,
        scratch_shapes=[pltpu.VMEM((PB, 2 * PB), f32)],
        compiler_params=pltpu.CompilerParams(vmem_limit_bytes=20 << 20),
        name="cholesky",
    )(pivots)


def fitting_kernel(pivot_ref, inv_ref, phi_ref, psi_ref, out_ref, work, peak):
    pa, pb = pivot_halves(pivot_ref)
    inv = inv_ref[...]

    def chunk(at, width):
        pair = mm_nt(pa, phi_ref[at, :]) * mm_nt(pb, psi_ref[at, :])
        fit = jnp.dot(inv, pair, precision=highest, preferred_element_type=f32)
        work[:, at] = fit
        return fit

    peak[...] = jnp.zeros_like(peak)

    @pl.loop(0, 7)
    def _(j):
        fit = jnp.abs(chunk(pl.ds(pl.multiple_of(j * 512, 512), 512), 512))
        best = peak[...]
        for t in range(4):
            best = jnp.maximum(best, fit[:, t * 128 : t * 128 + 128])
        peak[...] = best

    fit = jnp.abs(chunk(slice(3584, 4000), 416))
    best = peak[...]
    for t in range(3):
        best = jnp.maximum(best, fit[:, t * 128 : t * 128 + 128])
    best = jnp.max(best, axis=1, keepdims=True)
    best = jnp.maximum(best, jnp.max(fit[:, 384:], axis=1, keepdims=True))
    store_codes(out_ref, work, best)


def fitting_codes(pivots, inverse, phi, psi):
    return pl.pallas_call(
        fitting_kernel,
        out_shape=jax.ShapeDtypeStruct((PB, WIDE), jnp.int16),
        in_specs=[VMEM] * 4,
        out_specs=VMEM,
        scratch_shapes=[pltpu.VMEM((PB, WIDE), f32), pltpu.VMEM((PB, 128), f32)],
        compiler_params=pltpu.CompilerParams(vmem_limit_bytes=30 << 20),
        name="fitting",
    )(pivots, inverse, phi, psi)


def conv_kernel(h_ref, wx_ref, wxt_ref, hy_ref, in_ref, out_ref, wz, planes, lines, flat, peak):
    wz[...] = jnp.zeros_like(wz)
    for part in range(2):
        h = h_ref[part]
        for n in range(4):
            wz[part, n, 32 * n : 32 * n + 80, 0:128] = h
            wz[part, n, 32 * n + 80 : 32 * n + 160, 128:256] = h
    scale = scale_of(in_ref[:, 3968:4096].astype(jnp.int32)[:, CODE_LANE : CODE_LANE + 1]) * (
        1.0 / LEVELS
    )

    def z_forward(start, n, line):
        q = in_ref[:, pl.ds(start, 256)].astype(jnp.int32).astype(f32)
        high, low = split(q)
        out = (mm(high, wz[0, n]) + mm(low, wz[0, n]) + mm(high, wz[1, n])) * scale
        planes[line] = out[:, :128]
        planes[line + 1] = out[:, 128:]

    @pl.loop(0, 6)
    def _(g):
        for n in range(4):
            z_forward(pl.multiple_of(g * 640 + n * 128, 128), n, g * 8 + n * 2)

    z_forward(3840, 0, 48)

    def lhs3(w_ref, rows, data):
        high, low = split(data)
        first = mm(w_ref[...], high)
        return first[:rows] + first[rows:] + mm(w_ref[:rows], low)

    @pl.loop(0, ROWS // 2)
    def _(pair):
        for yy in range(5):
            parts = []
            for s in range(2):
                at = pl.ds(pl.multiple_of((pair * 2 + s) * 16, 16), 16)
                parts.append(
                    jnp.concatenate([planes[x * 5 + yy, at, :] for x in range(10)], axis=0)
                )
            out = lhs3(wx_ref, 160, jnp.concatenate(parts, axis=1))
            for s in range(2):
                y = (pair * 2 + s) * 5 + yy
                lines[pl.ds(pl.multiple_of(y * 160, 160), 160), :] = out[:, s * 128 : s * 128 + 128]

    def signed(index):
        return jnp.where(2 * index < N, index, index - N).astype(f32)

    ky = signed(lax.broadcasted_iota(jnp.int32, (N, 128), 0))
    kz = signed(lax.broadcasted_iota(jnp.int32, (N, 128), 1))
    base = ky * ky + kz * kz

    @pl.loop(0, N)
    def _(kx):
        ats = [pl.ds(kx * 2 + s, N, stride=160) for s in range(2)]
        data = jnp.concatenate([lines[at, :] for at in ats], axis=1)
        fx = signed(jnp.full((N, 128), kx, jnp.int32))
        squared = base + fx * fx
        factor = (4.0 / math.pi / (N * N * N)) / jnp.maximum(squared, 1.0)
        factor = jnp.where(squared > 0.5, factor, 0.0)
        out = lhs3(hy_ref, N, data) * jnp.concatenate([factor, factor], axis=1)
        out = lhs3(hy_ref, N, out)
        for s in range(2):
            lines[ats[s], :] = out[:, s * 128 : s * 128 + 128]

    @pl.loop(0, ROWS // 2)
    def _(pair):
        for yy in range(5):
            parts = []
            for s in range(2):
                y = (pair * 2 + s) * 5 + yy
                parts.append(lines[pl.ds(pl.multiple_of(y * 160, 160), 160), :])
            out = lhs3(wxt_ref, 160, jnp.concatenate(parts, axis=1))
            for s in range(2):
                at = pl.ds(pl.multiple_of((pair * 2 + s) * 16, 16), 16)
                for x in range(10):
                    planes[x * 5 + yy, at, :] = out[x * 16 : x * 16 + 16, s * 128 : s * 128 + 128]

    def z_backward(n, line):
        high, low = split(jnp.concatenate([planes[line], planes[line + 1]], axis=1))
        return mm_nt(high, wz[0, n]) + mm_nt(low, wz[0, n]) + mm_nt(high, wz[1, n])

    peak[...] = jnp.zeros_like(peak)

    def keep(start, value):
        flat[:, pl.ds(start, 128)] = value
        peak[...] = jnp.maximum(peak[...], jnp.abs(value))

    @pl.loop(0, 6)
    def _(g):
        start = pl.multiple_of(g * 640, 128)
        before = None
        for n in range(4):
            out = z_backward(n, g * 8 + n * 2)
            first = out[:, :128]
            keep(start + n * 128, first if before is None else first + before)
            before = out[:, 128:]
        keep(start + 512, before)

    out = z_backward(0, 48)
    keep(3840, out[:, :128])
    keep(3968, out[:, 128:])
    store_codes(out_ref, flat, jnp.max(peak[...], axis=1, keepdims=True))


def convolve(codes):
    h = hartley()
    padded = np.zeros((N, 128))
    padded[:, :N] = h
    h_parts = np.stack(split_np(padded))
    wx = np.zeros((N, 2, 10, COLS, 2))
    for f in range(2):
        wx[:, f, :, :, f] = h.reshape(N, COLS, 10).transpose(0, 2, 1)
    wx = wx.reshape(160, 160)
    return pl.pallas_call(
        conv_kernel,
        out_shape=jax.ShapeDtypeStruct((PB, WIDE), jnp.int16),
        in_specs=[VMEM] * 5,
        out_specs=VMEM,
        scratch_shapes=[
            pltpu.VMEM((2, 4, 256, 256), bf16),
            pltpu.VMEM((50, 256, 128), f32),
            pltpu.VMEM((N * 160, 128), f32),
            pltpu.VMEM((PB, WIDE), f32),
            pltpu.VMEM((PB, 128), f32),
        ],
        compiler_params=pltpu.CompilerParams(vmem_limit_bytes=50 << 20),
        name="convolve",
    )(
        jnp.asarray(h_parts),
        jnp.asarray(np.concatenate(split_np(wx))),
        jnp.asarray(np.concatenate(split_np(wx.T))),
        jnp.asarray(np.concatenate(split_np(h))),
        codes,
    )


def decode_kernel(in_ref, out_ref):
    scale = scale_of(in_ref[:, 3968:4096].astype(jnp.int32)[:, CODE_LANE : CODE_LANE + 1]) * (
        1.0 / LEVELS
    )

    @pl.loop(0, 31)
    def _(j):
        at = pl.ds(pl.multiple_of(j * 128, 128), 128)
        block = in_ref[:, at].astype(jnp.int32).astype(f32) * scale
        out_ref[at, :] = block.T

    block = in_ref[:, 3968:4096].astype(jnp.int32).astype(f32) * scale
    out_ref[3968:4000, :] = block.T[:32]


def decode(codes):
    return pl.pallas_call(
        decode_kernel,
        out_shape=jax.ShapeDtypeStruct((CELLS, PB), f32),
        in_specs=[VMEM],
        out_specs=VMEM,
        compiler_params=pltpu.CompilerParams(vmem_limit_bytes=20 << 20),
        name="decode",
    )(codes)


def exchange(codes):
    return lax.all_to_all(codes, ("row", "col"), split_axis=0, concat_axis=0, tiled=True)


def hadamard_gram(left, right, left_index, right_index):
    first = mm_nt(left[:, :PB], right[:, :PB])
    second = mm_nt(left[:, PB:], right[:, PB:])
    return first * second + shift_value * (left_index[:, None] == right_index[None, :]).astype(f32)


def on_device(phi, psi, points):
    col_index = lax.axis_index("col")
    row_index = lax.axis_index("row")
    plane_count, line_count, depth_count, orbital_count = phi.shape
    flat_phi = phi.reshape(CELLS, orbital_count)
    flat_psi = psi.reshape(CELLS, orbital_count)
    global_x = points // (N * N)
    global_y = points // N % N
    global_z = points % N
    local_cell = (
        (global_x - col_index * plane_count) * line_count + global_y - row_index * line_count
    ) * N + global_z
    own = jnp.concatenate(
        [jnp.take(flat_phi, local_cell, axis=0), jnp.take(flat_psi, local_cell, axis=0)], axis=1
    )
    pivots = pivots_everywhere(own)
    row_samples = lax.all_gather(own, "col", axis=0, tiled=True)
    moves = []
    for block in range(ROWS * COLS):
        moves.append((block, (block % ROWS) * COLS + block // ROWS))
    col_samples = lax.all_gather(
        lax.ppermute(own, ("row", "col"), moves), "row", axis=0, tiled=True
    )
    inverse = inverse_factor(pivots)
    codes = fitting_codes(pivots, inverse, flat_phi, flat_psi)
    potential = decode(exchange(convolve(exchange(codes))))
    potential = potential.reshape(plane_count, line_count, depth_count, PB)

    pivot = pivots.transpose(1, 0, 2, 3).reshape(PB, 2 * PB)
    row_block = NMU // ROWS
    col_block = NMU // COLS
    row_global = row_index * row_block + jnp.arange(row_block, dtype=jnp.int32)
    col_global = col_index * col_block + jnp.arange(col_block, dtype=jnp.int32)
    ids = jnp.arange(PB, dtype=jnp.int32)
    panel_rows = jnp.dot(
        hadamard_gram(row_samples, pivot, row_global, ids), inverse.T, precision=highest
    )
    panel_cols = jnp.dot(
        hadamard_gram(col_samples, pivot, col_global, ids), inverse.T, precision=highest
    )
    schur = hadamard_gram(row_samples, col_samples, row_global, col_global) - jnp.dot(
        panel_rows, panel_cols.T, precision=lax.Precision.HIGH
    )
    return (schur, panel_rows, potential)


def solution(mesh):
    in_specs = (P("col", "row", None, None), P("col", "row", None, None), P(("row", "col")))
    out_specs = (P("row", "col"), P("row", None), P("col", "row", None, None))
    return jax.shard_map(
        on_device, mesh=mesh, in_specs=in_specs, out_specs=out_specs, check_vma=False
    )
```

time: 828 us -> 238 us (0.29); the launches traced: 813 us -> 237 us
  waiting for transfers between devices: 410 us -> 47.3 us
  Pallas kernels: 0 us -> 109 us
  blocking collectives: 105 us -> 0 us
  matrix products: 109 us -> 18.1 us
  local copies, waits for them, and re-layouts: 98.3 us -> 23.4 us
  other arithmetic: 60.2 us -> 1.46 us
  starting transfers between devices: 14.5 us -> 24 us
    all_gather x1 -> x2, waiting for transfers between devices: 326 us -> 0.04 us  [the longest x1 0.02 us: on_device(): lax.all_gather(lax.ppermute(own, ('row', 'col'), moves), 'row', axis=0, t...]
    pallas_call x0 -> x5, Pallas kernels: none -> 109 us  [the longest x1 53.9 us: convolve(): pl.pallas_call(conv_kernel, out_shape=jax.ShapeDtypeStruct((PB, WIDE), jn...]
    all_to_all x2 -> x0, blocking collectives: 105 us -> none  [the longest x1 52.9 us: on_device(): lax.all_to_all(spectra, 'row', split_axis=3, concat_axis=2, tiled=True)]
    dot_general x38 -> x9, matrix products: 108 us -> 18.1 us  [the longest x6 10.8 us: mm_nt(): lax.dot_general(a, b, (((1,), (1,)), ((), ())), preferred_element_type=f32)]
    another operation x15 -> x0, other arithmetic: 55.8 us -> none  [the longest x6 33.9 us: on_device(): lower_factor = jnp.linalg.cholesky(corner)]
    all_to_all x2, waiting for transfers between devices: 83.3 us -> 43.5 us  [exchange(): lax.all_to_all(codes, ('row', 'col'), split_axis=0, concat_axis=0, tiled=...]
    slice x12 -> x0, local copies, waits for them, and re-layouts: 36.2 us -> none  [the longest x8 27 us: transform(): real_part = stacked[0]]
    squeeze x8 -> x0, local copies, waits for them, and re-layouts: 27 us -> none  [the longest x4 16.4 us: transform(): real_part = stacked[0]]
  transfers between devices with their start and end apart: 3 -> 5, of which waited for: 3 -> 3; matrix products, arithmetic and copies ran while one was open for 3% -> 8% of each run, Pallas kernels for 0% -> 43%
where the time goes in v1:
time: 238 us; the launch traced here: 237 us
  Pallas kernels  109 us (46%)
  waiting for transfers between devices  47.3 us (20%)
  starting transfers between devices  24 us (10%)
  local copies, waits for them, and re-layouts  23.4 us (10%)
  matrix products  18.1 us (8%)
  between operations  14.3 us (6%)
    pallas_call x1, Pallas kernels, convolve(): pl.pallas_call(conv_kernel, out_shape=jax.ShapeDtypeStruct((PB, WIDE), jn...  53.9 us
    all_to_all x2, waiting for transfers between devices, exchange(): lax.all_to_all(codes, ('row', 'col'), split_axis=0, concat_axis=0, tiled=...  43.5 us
    pallas_call x1, Pallas kernels, pivots_everywhere(): pl.pallas_call(pivot_kernel, out_shape=jax.ShapeDtypeStruct((COLS, 2, 16,...  27.3 us
    all_to_all x2, starting transfers between devices, exchange(): lax.all_to_all(codes, ('row', 'col'), split_axis=0, concat_axis=0, tiled=...  17.9 us
    all_to_all x4, local copies, waits for them, and re-layouts, exchange(): lax.all_to_all(codes, ('row', 'col'), split_axis=0, concat_axis=0, tiled=...  12.4 us
    pallas_call x1, Pallas kernels, inverse_factor(): pl.pallas_call(cholesky_kernel, out_shape=jax.ShapeDtypeStruct((PB, PB),...  11.6 us
    dot_general x6, matrix products, mm_nt(): lax.dot_general(a, b, (((1,), (1,)), ((), ())), preferred_element_type=f32)  10.8 us
    pallas_call x1, Pallas kernels, fitting_codes(): pl.pallas_call(fitting_kernel, out_shape=jax.ShapeDtypeStruct((PB, WIDE),...  8.24 us
  transfers between devices with their start and end apart: 5, of which 3 were waited for; matrix products, arithmetic and copies ran while one was open for 8% of the time, Pallas kernels for 43%

profile of v1, /device:TPU:1, one launch (start us, length us, event | category | flops | bytes accessed | tf_op | source)
XLA Modules:
  0.0 237.3 jit_solution(8736077109743924660)
XLA Ops:
  7.9 2.6 %gather_fusion = bf16[128,256]{1,0:T(8,128)(2,1)S(1)} fusion(bf16[4000,256]{1,0:T(8,128)(2,1)} %bitcast.12, s32[1024]{0:T(1024)S(1)} %pad_clamp_fusion), kind=kCustom, calls=%fused_computation.clone | custom fusion | bytes 131584 | tf_op jit(solution)/shard_map/jit(_take)/gather | solution.py:495
  10.5 2.6 %gather_fusion.1 = bf16[128,256]{1,0:T(8,128)(2,1)S(1)} fusion(bf16[4000,256]{1,0:T(8,128)(2,1)} %bitcast.14, s32[1024]{0:T(1024)S(1)} %pad_clamp_fusion), kind=kCustom, calls=%fused_computation.1.clone | custom fusion | bytes 131584 | tf_op jit(solution)/shard_map/jit(_take)/gather | solution.py:495
  13.9 6.0 %collective-permute-start = (bf16[128,512]{1,0:T(8,128)(2,1)}, bf16[128,512]{1,0:T(8,128)(2,1)S(1)}, u32[]{:S(2)}, u32[]{:S(2)}) collective-permute-start(bf16[128,512]{1,0:T(8,128)(2,1)} %pad_maximum_fusion.own_ref), channel_id=1, source_target_pairs={{0,0},{1,8},{2,16},{3,24},{4,32},{5,40},{6,48},{7,56},{8,64},{9,72... | collective-permute-start | bytes 393224 | tf_op jit(solution)/shard_map/ppermute | solution.py:503
  20.0 3.7 %collective-permute-done = bf16[128,512]{1,0:T(8,128)(2,1)S(1)} collective-permute-done((bf16[128,512]{1,0:T(8,128)(2,1)}, bf16[128,512]{1,0:T(8,128)(2,1)S(1)}, u32[]{:S(2)}, u32[]{:S(2)}) %collective-permute-start) | collective-permute-done | bytes 131104 | tf_op jit(solution)/shard_map/ppermute | solution.py:503
  24.4 27.3 %pivots.1.pivot_ref = bf16[8,2,16,512]{3,2,1,0:T(8,128)(2,1)} custom-call(bf16[128,512]{1,0:T(8,128)(2,1)} %pad_maximum_fusion.own_ref), custom_call_target="tpu_custom_call" | custom-call | tf_op jit(solution)/shard_map/pivots/pallas_call | solution.py:183
  52.6 11.6 %cholesky.1.inv_ref = f32[256,256]{1,0:T(8,128)S(1)} custom-call(bf16[8,2,16,512]{3,2,1,0:T(8,128)(2,1)S(1)} %copy-done), custom_call_target="tpu_custom_call" | custom-call | tf_op jit(solution)/shard_map/cholesky/pallas_call | solution.py:258
  65.2 1.6 copy-done.3
  66.8 1.6 copy-done.4
  68.3 8.2 %fitting.1 = s16[256,4096]{1,0:T(8,128)(2,1)S(1)} custom-call(bf16[8,2,16,512]{3,2,1,0:T(8,128)(2,1)S(1)} %copy-done.1, f32[256,256]{1,0:T(8,128)S(1)} %cholesky.1.inv_ref, bf16[4000,256]{1,0:T(8,128)(2,1)S(1)} %bitcast.13, bf16[4000,256]{1,0:T(8,128)(2,1)S(1)} %bitcast.15), custom_call_target="tpu_custom_call" | custom-call | tf_op jit(solution)/shard_map/fitting/pallas_call | solution.py:299
  76.6 2.7 %all_to_all.14 = s16[128,2,4096]{2,1,0:T(2,128)(2,1)} reshape(s16[256,4096]{1,0:T(8,128)(2,1)S(1)} %fitting.1) | data formatting | bytes 4194304 | tf_op jit(solution)/shard_map/all_to_all | solution.py:473
  79.3 13.2 %all-to-all-start = ((s16[128,2,4096]{2,1,0:T(2,128)(2,1)}), s16[128,2,4096]{2,1,0:T(2,128)(2,1)}, u32[]{:S(2)}, u32[]{:S(2)}) async-start(s16[128,2,4096]{2,1,0:T(2,128)(2,1)} %all_to_all.14), calls=%async_computation | async-start | bytes 4194304 | tf_op jit(solution)/shard_map/all_to_all | solution.py:473
  95.3 2.0 fusion.19
  97.4 27.0 %all-to-all-done = s16[128,2,4096]{2,1,0:T(2,128)(2,1)} async-done(((s16[128,2,4096]{2,1,0:T(2,128)(2,1)}), s16[128,2,4096]{2,1,0:T(2,128)(2,1)}, u32[]{:S(2)}, u32[]{:S(2)}) %all-to-all-start) | async-done | bytes 2097184 | tf_op jit(solution)/shard_map/all_to_all | solution.py:473
  124.3 4.1 %all_to_all.16.in_ref = s16[256,4096]{1,0:T(8,128)(2,1)} reshape(s16[128,2,4096]{2,1,0:T(2,128)(2,1)} %all-to-all-done) | data formatting | bytes 4194304 | tf_op jit(solution)/shard_map/all_to_all | solution.py:473
  128.5 53.9 %convolve.1 = s16[256,4096]{1,0:T(8,128)(2,1)S(1)} custom-call(bf16[2,80,128]{2,1,0:T(8,128)(2,1)S(1)} %copy-done.7, bf16[320,160]{1,0:T(8,128)(2,1)S(1)} %copy-done.5, bf16[320,160]{1,0:T(8,128)(2,1)S(1)} %copy-done.6, bf16[160,80]{1,0:T(8,128)(2,1)S(1)} %copy-done.8, s16[256,4096]{1,0:T(8,128)(2,1)} %all_to_all.16.in_ref), custom_call_target="tpu_custom_call" | custom-call | tf_op jit(solution)/shard_map/convolve/pallas_call | solution.py:423
  182.4 2.7 %all_to_all.17 = s16[128,2,4096]{2,1,0:T(2,128)(2,1)} reshape(s16[256,4096]{1,0:T(8,128)(2,1)S(1)} %convolve.1) | data formatting | bytes 4194304 | tf_op jit(solution)/shard_map/all_to_all | solution.py:473
  185.1 4.7 %all-to-all-start.1 = ((s16[128,2,4096]{2,1,0:T(2,128)(2,1)}), s16[128,2,4096]{2,1,0:T(2,128)(2,1)}, u32[]{:S(2)}, u32[]{:S(2)}) async-start(s16[128,2,4096]{2,1,0:T(2,128)(2,1)} %all_to_all.17), calls=%async_computation.1 | async-start | bytes 4194304 | tf_op jit(solution)/shard_map/all_to_all | solution.py:473
  189.9 1.8 fusion.2
  192.3 1.8 fusion.20
  195.5 3.5 %fusion.21 = f32[1024,2048]{1,0:T(8,128)S(1)} fusion(f32[1024,256]{1,0:T(8,128)S(1)} %copy-done.10, f32[2048,256]{1,0:T(8,128)S(1)} %fusion.20), kind=kOutput, calls=%fused_computation.40 | convolution fusion | flops 3221225472 | bytes 11534336 | tf_op jit(solution)/shard_map/dot_general | solution.py:522
  199.0 4.4 %add_subtract_fusion = f32[1024,2048]{1,0:T(8,128)} fusion(f32[1024,2048]{1,0:T(8,128)S(1)} %fusion.21, f32[1024,2048]{1,0:T(8,128)S(1)} %fusion.4, s32[2048]{0:T(1024)S(1)} %iota_add_fusion, s32[1024]{0:T(1024)S(1)} %iota_add_fusion.1, bf16[2048,512]{1,0:T(8,128)(2,1)S(1)} %copy-done.9, bf16[1024,512]{1,0:T(8,128)(2,1)S(1)} %copy-done.11), kind=kOutput, calls=%fused_computation.2 | convolution fusion | flops 1084227584 | bytes 26750976 | tf_op jit(solution)/shard_map/dot_general | solution.py:51
  203.4 16.6 %all-to-all-done.1 = s16[128,2,4096]{2,1,0:T(2,128)(2,1)} async-done(((s16[128,2,4096]{2,1,0:T(2,128)(2,1)}), s16[128,2,4096]{2,1,0:T(2,128)(2,1)}, u32[]{:S(2)}, u32[]{:S(2)}) %all-to-all-start.1) | async-done | bytes 2097184 | tf_op jit(solution)/shard_map/all_to_all | solution.py:473
  219.9 2.8 %all_to_all.19.in_ref = s16[256,4096]{1,0:T(8,128)(2,1)S(1)} reshape(s16[128,2,4096]{2,1,0:T(2,128)(2,1)} %all-to-all-done.1) | data formatting | bytes 4194304 | tf_op jit(solution)/shard_map/all_to_all | solution.py:473
  222.7 7.7 %decode.1 = f32[4000,256]{1,0:T(8,128)} custom-call(s16[256,4096]{1,0:T(8,128)(2,1)S(1)} %all_to_all.19.in_ref), custom_call_target="tpu_custom_call" | custom-call | tf_op jit(solution)/shard_map/decode/pallas_call | solution.py:462
  (41 shorter events, 8.9 us)
Async XLA Ops:
  7.2 85.4 %all-gather.3.cloned.1.call-start = ((), (), s32[]{:S(2)}) async-start(), calls=%async_computation.2 | async-start | bytes 1179648 | tf_op jit(solution)/shard_map/all_gather | solution.py:498
  13.9 175.9 %all-gather.5.cloned.1.call-start = ((), (), s32[]{:S(2)}) async-start(), calls=%async_computation.3 | async-start | bytes 2228224 | tf_op jit(solution)/shard_map/all_gather | solution.py:502
  13.9 9.7 %collective-permute-start = (bf16[128,512]{1,0:T(8,128)(2,1)}, bf16[128,512]{1,0:T(8,128)(2,1)S(1)}, u32[]{:S(2)}, u32[]{:S(2)}) collective-permute-start(bf16[128,512]{1,0:T(8,128)(2,1)} %pad_maximum_fusion.own_ref), channel_id=1, source_target_pairs={{0,0},{1,8},{2,16},{3,24},{4,32},{5,40},{6,48},{7,56},{8,64},{9,72... | collective-permute-start | bytes 393224 | tf_op jit(solution)/shard_map/ppermute | solution.py:503
  23.7 0.7 copy-start.12
  51.6 1.0 copy-start
  64.2 1.0 copy-start.1
  65.2 1.6 copy-start.3
  66.8 1.6 copy-start.4
  79.3 13.2 %copy-start.2 = (bf16[8,2,16,512]{3,2,1,0:T(8,128)(2,1)S(1)}, bf16[8,2,16,512]{3,2,1,0:T(8,128)(2,1)}, u32[]{:S(2)}) copy-start(bf16[8,2,16,512]{3,2,1,0:T(8,128)(2,1)} %pivots.1.pivot_ref) | copy-start | bytes 786436
  79.3 45.0 %all-to-all-start = ((s16[128,2,4096]{2,1,0:T(2,128)(2,1)}), s16[128,2,4096]{2,1,0:T(2,128)(2,1)}, u32[]{:S(2)}, u32[]{:S(2)}) async-start(s16[128,2,4096]{2,1,0:T(2,128)(2,1)} %all_to_all.14), calls=%async_computation | async-start | bytes 4194304 | tf_op jit(solution)/shard_map/all_to_all | solution.py:473
  97.3 31.1 %copy-start.5 = (bf16[320,160]{1,0:T(8,128)(2,1)S(1)}, bf16[320,160]{1,0:T(8,128)(2,1)}, u32[]{:S(2)}) copy-start(bf16[320,160]{1,0:T(8,128)(2,1)} %constant.75.clone.wx_ref) | copy-start | bytes 307204
  97.3 31.1 %copy-start.6 = (bf16[320,160]{1,0:T(8,128)(2,1)S(1)}, bf16[320,160]{1,0:T(8,128)(2,1)}, u32[]{:S(2)}) copy-start(bf16[320,160]{1,0:T(8,128)(2,1)} %constant.76.clone.wxt_ref) | copy-start | bytes 307204
  97.3 31.1 %copy-start.7 = (bf16[2,80,128]{2,1,0:T(8,128)(2,1)S(1)}, bf16[2,80,128]{2,1,0:T(8,128)(2,1)}, u32[]{:S(2)}) copy-start(bf16[2,80,128]{2,1,0:T(8,128)(2,1)} %constant.74.clone.h_ref) | copy-start | bytes 122884
  97.3 31.1 %copy-start.8 = (bf16[160,80]{1,0:T(8,128)(2,1)S(1)}, bf16[160,80]{1,0:T(8,128)(2,1)}, u32[]{:S(2)}) copy-start(bf16[160,80]{1,0:T(8,128)(2,1)} %constant.77.clone.hy_ref) | copy-start | bytes 76804
  185.1 34.8 %all-to-all-start.1 = ((s16[128,2,4096]{2,1,0:T(2,128)(2,1)}), s16[128,2,4096]{2,1,0:T(2,128)(2,1)}, u32[]{:S(2)}, u32[]{:S(2)}) async-start(s16[128,2,4096]{2,1,0:T(2,128)(2,1)} %all_to_all.17), calls=%async_computation.1 | async-start | bytes 4194304 | tf_op jit(solution)/shard_map/all_to_all | solution.py:473
  189.9 1.9 copy-start.9
  192.3 1.9 copy-start.11
  194.2 1.3 copy-start.10
Sparse Core Ops, SparseCore 0:
  14.0 48.8 all-gather.2
  65.1 53.6 all-gather.4

commit v2 on v0

v2 whole, which is shorter than its diff:
```python
import functools
import math

import jax
import jax.numpy as jnp
import numpy as np
from jax import lax
from jax.experimental import pallas as pl
from jax.experimental.pallas import tpu as pltpu
from jax.sharding import PartitionSpec as P

NMU = 16384
PB = 256
N = 80
ROWS = 16
COLS = 8
CELLS = 4000
WIDE = 4096
DEVICES = 128
WORDS = DEVICES * 16
CODE_LANE = 4000 - 31 * 128
LEVELS = 32766.0
LN2 = math.log(2.0)
shift_value = 4.0
highest = lax.Precision.HIGHEST
MESH = pl.DeviceIdType.MESH
VMEM = pl.BlockSpec(memory_space=pltpu.VMEM)
f32 = jnp.float32
bf16 = jnp.bfloat16


def hartley():
    angle = (np.outer(np.arange(N), np.arange(N)) % N) * (2.0 * np.pi / N)
    return np.cos(angle) + np.sin(angle)


def split_np(a):
    high = a.astype(np.float32).astype(jnp.bfloat16)
    low = (a - high.astype(np.float64)).astype(np.float32).astype(jnp.bfloat16)
    return high, low


def split(a):
    high = a.astype(bf16)
    return high, (a - high.astype(f32)).astype(bf16)


def mm(a, b):
    return jnp.dot(a, b, preferred_element_type=f32)


def mm_nt(a, b):
    return lax.dot_general(a, b, (((1,), (1,)), ((), ())), preferred_element_type=f32)


def encode(peak):
    code = jnp.ceil(jnp.log(jnp.maximum(peak, 1e-30)) * (256.0 / LN2))
    return code, jnp.exp(code * (LN2 / 256.0))


def words_of(low, high):
    return (low & 0xFFFF) | (high << 16)


def low_of(words):
    return ((words << 16) >> 16).astype(f32)


def high_of(words):
    return (words >> 16).astype(f32)


def quantize(values, factor):
    return jnp.clip(jnp.round(values * factor), -32767.0, 32767.0)


def store_codes(out_ref, source_ref, first, peak):
    code, scale = encode(peak)
    factor = LEVELS / scale
    rows = slice(first, first + 128)

    def tile(j):
        return quantize(source_ref[rows, pl.ds(j * 128, 128)], factor)

    def store(j, high):
        words = words_of(tile(j).astype(jnp.int32), high.astype(jnp.int32))
        out_ref[pl.ds(j, 128, stride=16), :] = words

    @pl.loop(0, 5)
    def _(group):
        for t in range(3):
            j = pl.multiple_of(group * 3, 1) + t
            store(j, tile(j + 16))

    last = tile(31)
    lane = lax.broadcasted_iota(jnp.int32, last.shape, 1)
    store(15, jnp.where(lane < CODE_LANE, last, jnp.where(lane == CODE_LANE, code, 0.0)))


def load_scale(in_ref):
    last = high_of(in_ref[pl.ds(15, 128, stride=16), :])
    return jnp.exp(last[:, CODE_LANE : CODE_LANE + 1] * (LN2 / 256.0)) * (1.0 / LEVELS)


def pivot_halves(pivot_ref):
    rows = [pivot_ref[:, owner].reshape(128, 2 * PB) for owner in range(2)]
    both = jnp.concatenate(rows, axis=0)
    return both[:, :PB], both[:, PB:]


def invert_factor(pa, pb, inv_ref, w):
    i0 = lax.broadcasted_iota(jnp.int32, (PB, PB), 0)
    i1 = lax.broadcasted_iota(jnp.int32, (PB, PB), 1)
    eye = (i0 == i1).astype(f32)
    w[:, :PB] = mm_nt(pa, pa) * mm_nt(pb, pb) + shift_value * eye
    w[:, PB:] = eye
    nb = 32
    for block in range(PB // nb):
        g = block * nb
        panel = w[g : g + nb, :]
        sub = lax.broadcasted_iota(jnp.int32, (nb, 128), 0)
        for j in range(0, nb, 8):
            cols = [
                jnp.broadcast_to(panel[:, g + j + t : g + j + t + 1], (nb, 128)) for t in range(8)
            ]
            for t in range(8):
                k = j + t
                pivot = jnp.broadcast_to(cols[t][k : k + 1, :], (nb, 128))
                root = lax.rsqrt(pivot)
                root = root * (1.5 - 0.5 * pivot * root * root)
                left = cols[t] * root
                for u in range(t + 1, 8):
                    cols[u] = cols[u] - left * jnp.broadcast_to(
                        left[j + u : j + u + 1, :], (nb, 128)
                    )
                below = jnp.where(sub > k, left, 0.0)
                below = jnp.where(sub == k, 1.0 - root, below)
                wide = jnp.concatenate([below] * 4, axis=1)
                line = jnp.broadcast_to(panel[k : k + 1, :], (nb, 2 * PB))
                scaled = line * jnp.concatenate([root] * 4, axis=1)
                row_k = jnp.concatenate([sub == k] * 4, axis=1)
                panel = jnp.where(row_k, scaled, panel - wide * scaled)
        w[g : g + nb, :] = panel
        if g + nb < PB:
            left = panel[:, g + nb : PB] if (g + nb) % 128 == 0 else panel[:, :PB]
            if (g + nb) % 128 == 0:
                update = lax.dot_general(
                    left, panel, (((0,), (0,)), ((), ())), precision=highest, preferred_element_type=f32
                )
                w[g + nb :, :] = w[g + nb :, :] - update
            else:
                update = lax.dot_general(
                    left, panel, (((0,), (0,)), ((), ())), precision=highest, preferred_element_type=f32
                )
                w[g + nb :, :] = w[g + nb :, :] - update[g + nb :, :]
    inv_ref[...] = jnp.where(i0 >= i1, w[:, PB:], 0.0)


def fit(pa, pb, inv, phi, psi, out_ref, work, peak):
    def chunk(at):
        pair = mm_nt(pa, phi[at, :]) * mm_nt(pb, psi[at, :])
        fitted = jnp.dot(inv, pair, precision=highest, preferred_element_type=f32)
        work[:, at] = fitted
        return jnp.abs(fitted)

    peak[...] = jnp.zeros_like(peak)

    @pl.loop(0, 7)
    def _(j):
        fitted = chunk(pl.ds(pl.multiple_of(j * 512, 512), 512))
        best = peak[...]
        for t in range(4):
            best = jnp.maximum(best, fitted[:, t * 128 : t * 128 + 128])
        peak[...] = best

    fitted = chunk(slice(3584, 4000))
    best = peak[...]
    for t in range(3):
        best = jnp.maximum(best, fitted[:, t * 128 : t * 128 + 128])
    best = jnp.max(best, axis=1, keepdims=True)
    best = jnp.maximum(best, jnp.max(fitted[:, 384:], axis=1, keepdims=True))
    for f in range(2):
        store_codes(out_ref.at[f], work, f * 128, best[f * 128 : f * 128 + 128])


def head_kernel(
    own_ref, phi_ref, psi_ref,
    out_ref, pivot_ref, inv_ref, rows_ref, cols_ref,
    phi, psi, w, work, peak, send1, recv1, send2, recv2, send3, recv3,
    send_row, recv_row, send_move, recv_move, send_col, recv_col, send_core, recv_core, local,
):
    r = lax.axis_index("row")
    c = lax.axis_index("col")
    half = r // 2
    core = lax.rem(r, 2)
    goal_row = 8 * core + c
    goal_col = half
    stays = (goal_row == r) & (goal_col == c)
    source_row = 2 * c + r // 8
    source_col = lax.rem(r, 8)

    def at(row, col):
        return {"row": row, "col": col}

    def remote(source, target, send, recv, device):
        return pltpu.make_async_remote_copy(
            source, target, send, recv, device_id=device, device_id_type=MESH
        )

    loads = [
        pltpu.make_async_copy(phi_ref, phi, local.at[0]),
        pltpu.make_async_copy(psi_ref, psi, local.at[1]),
    ]
    for load in loads:
        load.start()

    barrier = pltpu.get_barrier_semaphore()
    for d in range(1, COLS):
        pl.semaphore_signal(
            barrier, inc=1, device_id=at(r, lax.rem(c + d, COLS)), device_id_type=MESH
        )
    for d in range(1, ROWS):
        pl.semaphore_signal(
            barrier, inc=1, device_id=at(lax.rem(r + d, ROWS), c), device_id_type=MESH
        )

    @pl.when(jnp.logical_not(stays))
    def _():
        for device in (at(goal_row, goal_col), at(source_row, source_col)):
            pl.semaphore_signal(barrier, inc=1, device_id=device, device_id_type=MESH)
        pl.semaphore_wait(barrier, COLS + ROWS)

    @pl.when(stays)
    def _():
        pl.semaphore_wait(barrier, COLS + ROWS - 2)

    def scatter(owner, j):
        return remote(
            own_ref.at[pl.ds(pl.multiple_of(j * 16, 16), 16)],
            pivot_ref.at[j, owner],
            send1.at[j],
            recv1.at[owner],
            at(0, j),
        )

    for owner in range(2):

        @pl.when((r == 0) & (c == owner))
        def _():
            keep = pltpu.make_async_copy(
                own_ref.at[pl.ds(owner * 16, 16)], pivot_ref.at[owner, owner], local.at[2]
            )
            keep.start()
            for d in range(1, COLS):
                scatter(owner, (owner + d) % COLS).start()
            keep.wait()

        @pl.when((r == 0) & (c != owner))
        def _():
            scatter(owner, c).wait_recv()

    def down(d):
        return remote(pivot_ref.at[c], pivot_ref.at[c], send2.at[d], recv2, at(d, c))

    @pl.when(r == 0)
    def _():
        for d in range(1, ROWS):
            down(d).start()

    @pl.when(r != 0)
    def _():
        down(1).wait_recv()

    def across(d):
        return remote(
            pivot_ref.at[c], pivot_ref.at[c], send3.at[d], recv3.at[d], at(r, lax.rem(c + d, COLS))
        )

    for d in range(1, COLS):
        across(d).start()
    for d in range(1, COLS):
        source = lax.rem(c + COLS - d, COLS)
        remote(
            pivot_ref.at[source], pivot_ref.at[source], send3.at[d], recv3.at[d], at(r, source)
        ).wait_recv()

    keep_rows = pltpu.make_async_copy(own_ref, rows_ref.at[c], local.at[3])
    keep_rows.start()
    move = remote(own_ref, cols_ref.at[goal_row], send_move, recv_move, at(goal_row, goal_col))
    keep_move = pltpu.make_async_copy(own_ref, cols_ref.at[goal_row], local.at[4])

    @pl.when(jnp.logical_not(stays))
    def _():
        move.start()

    @pl.when(stays)
    def _():
        keep_move.start()

    def row_send(d):
        return remote(
            own_ref, rows_ref.at[c], send_row.at[d], recv_row.at[d], at(r, lax.rem(c + d, COLS))
        )

    for d in range(1, COLS):
        row_send(d).start()

    pa, pb = pivot_halves(pivot_ref)
    invert_factor(pa, pb, inv_ref, w)

    @pl.when(jnp.logical_not(stays))
    def _():
        remote(
            own_ref, cols_ref.at[r], send_move, recv_move, at(source_row, source_col)
        ).wait_recv()

    @pl.when(stays)
    def _():
        keep_move.wait()

    def col_send(d):
        return remote(
            cols_ref.at[r],
            cols_ref.at[r],
            send_col.at[d],
            recv_col.at[d],
            at(lax.rem(half + d, COLS) * 2 + core, c),
        )

    for d in range(1, COLS):
        col_send(d).start()

    def core_send(d):
        block = lax.rem(half + COLS - d, COLS) * 2 + core
        return remote(
            cols_ref.at[block],
            cols_ref.at[block],
            send_core.at[d],
            recv_core.at[d],
            at(half * 2 + 1 - core, c),
        )

    core_send(0).start()
    for load in loads:
        load.wait()
    fit(pa, pb, inv_ref[...], phi, psi, out_ref, work, peak)

    for d in range(1, COLS):
        block = lax.rem(half + COLS - d, COLS) * 2 + core
        remote(
            cols_ref.at[block], cols_ref.at[block], send_col.at[d], recv_col.at[d], at(block, c)
        ).wait_recv()
        core_send(d).start()
    keep_rows.wait()
    for d in range(1, COLS):
        source = lax.rem(c + COLS - d, COLS)
        remote(
            own_ref, rows_ref.at[source], send_row.at[d], recv_row.at[d], at(r, source)
        ).wait_recv()
    for d in range(COLS):
        block = lax.rem(half + COLS - d, COLS) * 2 + 1 - core
        remote(
            cols_ref.at[block],
            cols_ref.at[block],
            send_core.at[d],
            recv_core.at[d],
            at(half * 2 + 1 - core, c),
        ).wait_recv()

    @pl.when(jnp.logical_not(stays))
    def _():
        move.wait_send()

    for d in range(1, COLS):
        across(d).wait_send()
        row_send(d).wait_send()
        col_send(d).wait_send()
    for d in range(COLS):
        core_send(d).wait_send()

    @pl.when(r == 0)
    def _():
        for d in range(1, ROWS):
            down(d).wait_send()

    for owner in range(2):

        @pl.when((r == 0) & (c == owner))
        def _():
            for d in range(1, COLS):
                scatter(owner, (owner + d) % COLS).wait_send()


def head(own, phi, psi):
    dma = pltpu.SemaphoreType.DMA
    anywhere = pl.BlockSpec(memory_space=pl.ANY)
    return pl.pallas_call(
        head_kernel,
        out_shape=(
            jax.ShapeDtypeStruct((2, WORDS, 128), jnp.int32),
            jax.ShapeDtypeStruct((COLS, 2, 16, 2 * PB), bf16),
            jax.ShapeDtypeStruct((PB, PB), f32),
            jax.ShapeDtypeStruct((COLS, 128, 2 * PB), bf16),
            jax.ShapeDtypeStruct((ROWS, 128, 2 * PB), bf16),
        ),
        in_specs=[VMEM, anywhere, anywhere],
        out_specs=(VMEM,) * 5,
        scratch_shapes=[
            pltpu.VMEM((CELLS, PB), bf16),
            pltpu.VMEM((CELLS, PB), bf16),
            pltpu.VMEM((PB, 2 * PB), f32),
            pltpu.VMEM((PB, WIDE), f32),
            pltpu.VMEM((PB, 128), f32),
            dma((COLS,)),
            dma((2,)),
            dma((ROWS,)),
            dma,
            dma((COLS,)),
            dma((COLS,)),
            dma((COLS,)),
            dma((COLS,)),
            dma,
            dma,
            dma((COLS,)),
            dma((COLS,)),
            dma((COLS,)),
            dma((COLS,)),
            dma((5,)),
        ],
        compiler_params=pltpu.CompilerParams(
            collective_id=1, has_side_effects=True, vmem_limit_bytes=60 << 20
        ),
        name="head",
    )(own, phi, psi)


def half_convolution(f, hx, hxt, hy, wz, wzt, got, sent, high, low, planes, lines, flat, peak):
    scale = load_scale(got)

    @pl.loop(0, 4)
    def _(group):
        for t in range(4):
            j = group * 4 + t
            words = got[pl.ds(j, 128, stride=16), :]
            for s, value in enumerate((low_of(words), high_of(words))):
                at = pl.ds(pl.multiple_of((j + 16 * s) * 128, 128), 128)
                high[:, at], low[:, at] = split(value)

    def z_forward(n, start, line):
        at = pl.ds(start, 256)
        first = high[:, at]
        out = mm(jnp.concatenate([first, low[:, at], first], axis=1), wz[n]) * scale
        planes[line] = out[:, :128]
        planes[line + 1] = out[:, 128:]

    @pl.loop(0, 6)
    def _(g):
        for n in range(4):
            z_forward(n, pl.multiple_of(g * 640 + n * 128, 128), g * 8 + n * 2)

    z_forward(0, 3840, 48)

    def mm3(w, data):
        first, second = split(data)
        return mm(w, jnp.concatenate([first, first, second], axis=0))

    def both(value):
        return value[:, :128], value[:, 128:]

    def line_at(y):
        return pl.ds(pl.multiple_of(y * N, 16), N)

    @pl.loop(0, ROWS // 2)
    def _(pair):
        for yy in range(5):
            halves = []
            for s in range(2):
                at = pl.ds(pl.multiple_of((pair * 2 + s) * 8, 8), 8)
                halves.append(
                    jnp.concatenate([planes[x * 5 + yy, at, :] for x in range(10)], axis=0)
                )
            out = both(mm3(hx, jnp.concatenate(halves, axis=1)))
            for s in range(2):
                lines[line_at((pair * 2 + s) * 5 + yy), :] = out[s]

    def signed(index):
        return jnp.where(2 * index < N, index, index - N).astype(f32)

    ky = signed(lax.broadcasted_iota(jnp.int32, (N, 128), 0))
    kz = signed(lax.broadcasted_iota(jnp.int32, (N, 128), 1))
    base = ky * ky + kz * kz

    @pl.loop(0, N // 8)
    def _(group):
        ats = [pl.ds(group * 8 + t, N, stride=N) for t in range(8)]
        datas = [lines[at, :] for at in ats]
        outs = []
        for t in range(0, 8, 2):
            factors = []
            for s in range(2):
                fx = signed(jnp.full((N, 128), group * 8 + t + s, jnp.int32))
                squared = base + fx * fx
                factor = (4.0 / math.pi / (N * N * N)) / jnp.maximum(squared, 1.0)
                factors.append(jnp.where(squared > 0.5, factor, 0.0))
            out = mm3(hy, jnp.concatenate(datas[t : t + 2], axis=1))
            outs.extend(both(mm3(hy, out * jnp.concatenate(factors, axis=1))))
        for at, out in zip(ats, outs, strict=True):
            lines[at, :] = out

    @pl.loop(0, ROWS // 2)
    def _(pair):
        for yy in range(5):
            halves = [lines[line_at((pair * 2 + s) * 5 + yy), :] for s in range(2)]
            out = both(mm3(hxt, jnp.concatenate(halves, axis=1)))
            for s in range(2):
                at = pl.ds(pl.multiple_of((pair * 2 + s) * 8, 8), 8)
                for x in range(10):
                    planes[x * 5 + yy, at, :] = out[s][x * 8 : x * 8 + 8]

    def z_backward(n, line):
        first = split(planes[line])
        second = split(planes[line + 1])
        data = jnp.concatenate(
            [first[0], second[0], first[1], second[1], first[0], second[0]], axis=1
        )
        return both(mm_nt(data, wzt[n]))

    peak[...] = jnp.zeros_like(peak)

    @pl.loop(0, 6)
    def _(g):
        start = pl.multiple_of(g * 640, 128)
        best = peak[...]
        before = None
        for n in range(5):
            value = before
            if n < 4:
                out, after = z_backward(n, g * 8 + n * 2)
                value = out if before is None else out + before
                before = after
            flat[:, pl.ds(start + n * 128, 128)] = value
            best = jnp.maximum(best, jnp.abs(value))
        peak[...] = best

    best = peak[...]
    for t, value in enumerate(z_backward(0, 48)):
        flat[:, 3840 + t * 128 : 3968 + t * 128] = value
        best = jnp.maximum(best, jnp.abs(value))
    store_codes(sent, flat, 0, jnp.max(best, axis=1, keepdims=True))


def grams(left, right):
    return mm_nt(left[:, :PB], right[:, :PB]) * mm_nt(left[:, PB:], right[:, PB:])


def schur_tiles(pivot_ref, inv_ref, rows_ref, cols_ref, schur_ref, panel_ref, left3, right3, tiles, out_sem, r, c):
    pa, pb = pivot_halves(pivot_ref)
    pivots = jnp.concatenate([pa, pb], axis=1)
    inv = inv_ref[...]

    def shifted(gram, row, column):
        i = row + lax.broadcasted_iota(jnp.int32, gram.shape, 0)
        j = column + lax.broadcasted_iota(jnp.int32, gram.shape, 1)
        return gram + jnp.where(i == j, shift_value, 0.0)

    def panel_of(samples, row):
        return lax.dot_general(
            shifted(grams(samples, pivots), row, 0), inv, (((1,), (1,)), ((), ())),
            precision=highest, preferred_element_type=f32,
        )

    @pl.loop(0, 4)
    def _(i):
        at = pl.ds(pl.multiple_of(i * 256, 256), 256)
        panel = panel_of(rows_ref[at, :], r * 1024 + i * 256)
        panel_ref[at, :] = panel
        high, low = split(panel)
        left3[at, :] = jnp.concatenate([high, low, high], axis=1)

    @pl.loop(0, 8)
    def _(i):
        at = pl.ds(pl.multiple_of(i * 256, 256), 256)
        high, low = split(panel_of(cols_ref[at, :], c * 2048 + i * 256))
        right3[at, :] = jnp.concatenate([high, high, low], axis=1)

    def put(i, slot):
        return pltpu.make_async_copy(
            tiles.at[slot], schur_ref.at[pl.ds(pl.multiple_of(i * 128, 128), 128)], out_sem.at[slot]
        )

    @pl.loop(0, 4)
    def _(pair):
        for slot in range(2):
            i = pair * 2 + slot

            @pl.when(pair > 0)
            def _():
                put(i - 2, slot).wait()

            at = pl.ds(pl.multiple_of(i * 128, 128), 128)
            rows = rows_ref[at, :]
            left = left3[at, :]
            for j in range(4):
                cols = slice(j * 512, j * 512 + 512)
                gram = shifted(
                    grams(rows, cols_ref[cols, :]), r * 1024 + i * 128, c * 2048 + j * 512
                )
                tiles[slot, :, cols] = gram - mm_nt(left, right3[cols, :])
            put(i, slot).start()

    for slot in range(2):
        put(6 + slot, slot).wait()


def middle_kernel(
    h_ref, hx_ref, hxt_ref, hy_ref, codes_ref, pivot_ref, inv_ref, rows_ref, cols_ref,
    back_ref, panel_ref, schur_ref,
    got, sent, wz, wzt, high, low, planes, lines, flat, peak, left3, right3, tiles,
    send_there, recv_there, send_back, recv_back, own_sem, out_sem,
):
    r = lax.axis_index("row")
    c = lax.axis_index("col")
    me = r * COLS + c

    def at(i):
        device = lax.rem(me + i, DEVICES)
        return device, {"row": device // COLS, "col": lax.rem(device, COLS)}

    def block(i):
        return pl.ds(pl.multiple_of(i * 16, 16), 16)

    barrier = pltpu.get_barrier_semaphore()

    @pl.loop(1, DEVICES)
    def _(i):
        pl.semaphore_signal(barrier, inc=1, device_id=at(i)[1], device_id_type=MESH)

    pl.semaphore_wait(barrier, DEVICES - 1)

    def send_all(source, target, send, recv, keep):
        pltpu.make_async_copy(source.at[block(me)], target.at[block(me)], keep).start()

        @pl.loop(1, DEVICES)
        def _(i):
            device, where = at(i)
            pltpu.make_async_remote_copy(
                source.at[block(device)],
                target.at[block(me)],
                send,
                recv,
                device_id=where,
                device_id_type=MESH,
            ).start()

    def wait_all(ref, sem):
        most = ref.at[pl.ds(0, WORDS - 16)]
        pltpu.make_async_copy(most, most, sem).wait()

    def wait_own(source, target, keep):
        pltpu.make_async_copy(source.at[block(me)], target.at[block(me)], keep).wait()

    for f in range(2):
        send_all(codes_ref.at[f], got.at[f], send_there.at[f], recv_there.at[f], own_sem.at[f])

    wz[...] = jnp.zeros_like(wz)
    wzt[...] = jnp.zeros_like(wzt)
    for part, which in enumerate((0, 0, 1)):
        h = h_ref[which]
        for n in range(4):
            for s in range(2):
                first = 32 * n + 80 * s
                wz[n, part * 256 + first : part * 256 + first + 80, 128 * s : 128 * s + 128] = h
                lane = part * 256 + 128 * s
                wzt[n, first : first + 80, lane : lane + 128] = h

    schur_tiles(
        pivot_ref, inv_ref, rows_ref, cols_ref, schur_ref, panel_ref, left3, right3, tiles, out_sem, r, c
    )
    matrices = (hx_ref[...], hxt_ref[...], hy_ref[...])
    for f in range(2):
        wait_own(codes_ref.at[f], got.at[f], own_sem.at[f])
        wait_all(got.at[f], recv_there.at[f])
        half_convolution(
            f, *matrices, wz, wzt, got.at[f], sent.at[f], high, low, planes, lines, flat, peak
        )
        send_all(sent.at[f], back_ref.at[f], send_back.at[f], recv_back.at[f], own_sem.at[2 + f])
    for f in range(2):
        wait_own(sent.at[f], back_ref.at[f], own_sem.at[2 + f])
        wait_all(back_ref.at[f], recv_back.at[f])
    for f in range(2):
        wait_all(codes_ref.at[f], send_there.at[f])
        wait_all(sent.at[f], send_back.at[f])


def side_by_side(a):
    high, low = split_np(a)
    return jnp.asarray(np.concatenate([high, low, high], axis=1))


def middle(codes, pivots, inverse, rows, cols):
    h = hartley()
    padded = np.zeros((N, 128))
    padded[:, :N] = h
    h_parts = np.stack(split_np(padded))
    hx = h.reshape(N, COLS, 10).transpose(0, 2, 1).reshape(N, N)
    dma = pltpu.SemaphoreType.DMA
    return pl.pallas_call(
        middle_kernel,
        out_shape=(
            jax.ShapeDtypeStruct((2, WORDS, 128), jnp.int32),
            jax.ShapeDtypeStruct((NMU // ROWS, PB), f32),
            jax.ShapeDtypeStruct((NMU // ROWS, NMU // COLS), f32),
        ),
        in_specs=[VMEM] * 9,
        out_specs=(VMEM, VMEM, pl.BlockSpec(memory_space=pl.ANY)),
        scratch_shapes=[
            pltpu.VMEM((2, WORDS, 128), jnp.int32),
            pltpu.VMEM((2, WORDS, 128), jnp.int32),
            pltpu.VMEM((4, 768, 256), bf16),
            pltpu.VMEM((4, 256, 768), bf16),
            pltpu.VMEM((128, WIDE), bf16),
            pltpu.VMEM((128, WIDE), bf16),
            pltpu.VMEM((50, 128, 128), f32),
            pltpu.VMEM((N * N, 128), f32),
            pltpu.VMEM((128, WIDE), f32),
            pltpu.VMEM((128, 128), f32),
            pltpu.VMEM((NMU // ROWS, 768), bf16),
            pltpu.VMEM((NMU // COLS, 768), bf16),
            pltpu.VMEM((2, 128, NMU // COLS), f32),
            dma((2,)),
            dma((2,)),
            dma((2,)),
            dma((2,)),
            dma((4,)),
            dma((2,)),
        ],
        compiler_params=pltpu.CompilerParams(
            collective_id=2, has_side_effects=True, vmem_limit_bytes=60 << 20
        ),
        name="middle",
    )(
        jnp.asarray(h_parts),
        side_by_side(hx),
        side_by_side(hx.T),
        side_by_side(h),
        codes,
        pivots,
        inverse,
        rows,
        cols,
    )


def decode_kernel(in_ref, out_ref):
    for f in range(2):
        words_ref = in_ref.at[f]
        scale = load_scale(words_ref)
        lanes = slice(f * 128, f * 128 + 128)

        def put(tile, value):
            block = (value * scale).T
            at = pl.ds(pl.multiple_of(tile * 128, 128), 128)
            out_ref[at, lanes] = block

        @pl.loop(0, 5)
        def _(group):
            for t in range(3):
                words = words_ref[pl.ds(group * 3 + t, 128, stride=16), :]
                put(group * 3 + t, low_of(words))
                put(group * 3 + t + 16, high_of(words))

        words = words_ref[pl.ds(15, 128, stride=16), :]
        put(15, low_of(words))
        out_ref[3968:4000, lanes] = (high_of(words) * scale).T[:32]


def decode(codes):
    return pl.pallas_call(
        decode_kernel,
        out_shape=jax.ShapeDtypeStruct((CELLS, PB), f32),
        in_specs=[VMEM],
        out_specs=VMEM,
        compiler_params=pltpu.CompilerParams(vmem_limit_bytes=20 << 20),
        name="decode",
    )(codes)


def on_device(phi, psi, points):
    col_index = lax.axis_index("col")
    row_index = lax.axis_index("row")
    plane_count, line_count, depth_count, orbital_count = phi.shape
    flat_phi = phi.reshape(CELLS, orbital_count)
    flat_psi = psi.reshape(CELLS, orbital_count)
    global_x = points // (N * N)
    global_y = points // N % N
    global_z = points % N
    local_cell = (
        (global_x - col_index * plane_count) * line_count + global_y - row_index * line_count
    ) * N + global_z
    own = jnp.concatenate(
        [jnp.take(flat_phi, local_cell, axis=0), jnp.take(flat_psi, local_cell, axis=0)], axis=1
    )
    codes, pivots, inverse, row_samples, col_samples = head(own, flat_phi, flat_psi)
    row_samples = row_samples.reshape(NMU // ROWS, 2 * PB)
    col_samples = col_samples.reshape(NMU // COLS, 2 * PB)
    back, panel, schur = middle(codes, pivots, inverse, row_samples, col_samples)
    potential = decode(back).reshape(plane_count, line_count, depth_count, PB)
    return (schur, panel, potential)


def solution(mesh):
    in_specs = (P("col", "row", None, None), P("col", "row", None, None), P(("row", "col")))
    out_specs = (P("row", "col"), P("row", None), P("col", "row", None, None))
    return jax.shard_map(
        on_device, mesh=mesh, in_specs=in_specs, out_specs=out_specs, check_vma=False
    )
```

time: 828 us -> 175 us (0.21); the launches traced: 813 us -> 175 us
  waiting for transfers between devices: 410 us -> 0 us
  Pallas kernels: 0 us -> 157 us
  matrix products: 109 us -> 0 us
  blocking collectives: 105 us -> 0 us
  local copies, waits for them, and re-layouts: 98.3 us -> 15.7 us
  other arithmetic: 60.2 us -> 1.45 us
  between operations: 16.6 us -> 0.68 us
  starting transfers between devices: 14.5 us -> 0 us
    all_gather x1 -> x0, waiting for transfers between devices: 326 us -> none  [on_device(): lax.all_gather(own_samples, ('row', 'col'), axis=1, tiled=True)]
    pallas_call x0 -> x3, Pallas kernels: none -> 157 us  [the longest x1 90.5 us: middle(): pl.pallas_call(middle_kernel, out_shape=(jax.ShapeDtypeStruct((2, WORDS,...]
    dot_general x38 -> x0, matrix products: 108 us -> none  [the longest x6 29.7 us: transform(): cos_real = jnp.einsum(form, cosine, real_part, precision=highest)]
    all_to_all x2 -> x0, blocking collectives: 105 us -> none  [the longest x1 52.9 us: on_device(): lax.all_to_all(spectra, 'row', split_axis=3, concat_axis=2, tiled=True)]
    all_to_all x2 -> x0, waiting for transfers between devices: 83.3 us -> none  [the longest x1 57.4 us: on_device(): lax.all_to_all(spectra, 'col', split_axis=2, concat_axis=1, tiled=True)]
    another operation x15 -> x0, other arithmetic: 55.8 us -> none  [the longest x6 33.9 us: on_device(): lower_factor = jnp.linalg.cholesky(corner)]
    slice x12 -> x0, local copies, waits for them, and re-layouts: 36.2 us -> none  [the longest x8 27 us: transform(): real_part = stacked[0]]
    squeeze x8 -> x0, local copies, waits for them, and re-layouts: 27 us -> none  [the longest x4 16.4 us: transform(): real_part = stacked[0]]
  transfers between devices with their start and end apart: 3 -> 0, of which waited for: 3 -> 0; matrix products, arithmetic and copies ran while one was open for 3% -> 0% of each run, Pallas kernels for 0% -> 0%
where the time goes in v2:
time: 175 us
  Pallas kernels  157 us (90%)
  local copies, waits for them, and re-layouts  15.7 us (9%)
    pallas_call x1, Pallas kernels, middle(): pl.pallas_call(middle_kernel, out_shape=(jax.ShapeDtypeStruct((2, WORDS,...  90.5 us
    pallas_call x1, Pallas kernels, head(): pl.pallas_call(head_kernel, out_shape=(jax.ShapeDtypeStruct((2, WORDS, 12...  62 us
    unnamed x6, local copies, waits for them, and re-layouts  10.5 us
    pallas_call x1, Pallas kernels, decode(): pl.pallas_call(decode_kernel, out_shape=jax.ShapeDtypeStruct((CELLS, PB),...  4.69 us

profile of v2, /device:TPU:1, one launch (start us, length us, event | category | flops | bytes accessed | tf_op | source)
XLA Modules:
  0.0 175.0 jit_solution(7025931431212840125)
XLA Ops:
  0.6 0.7 compare_and_fusion
  1.3 2.6 %gather_fusion.1 = bf16[128,256]{1,0:T(8,128)(2,1)S(1)} fusion(bf16[4000,256]{1,0:T(8,128)(2,1)} %bitcast.8, s32[1024]{0:T(1024)S(1)} %pad_clamp_fusion), kind=kCustom, calls=%fused_computation.1.clone | custom fusion | bytes 131584 | tf_op jit(solution)/shard_map/jit(_take)/gather | solution.py:801
  3.9 2.6 %gather_fusion = bf16[128,256]{1,0:T(8,128)(2,1)S(1)} fusion(bf16[4000,256]{1,0:T(8,128)(2,1)} %bitcast.6, s32[1024]{0:T(1024)S(1)} %pad_clamp_fusion), kind=kCustom, calls=%fused_computation.clone | custom fusion | bytes 131584 | tf_op jit(solution)/shard_map/jit(_take)/gather | solution.py:801
  6.5 0.1 broadcast_select_fusion.1
  6.6 0.7 pad_maximum_fusion.own_ref
  7.3 62.0 %head.1 = (s32[2,2048,128]{2,1,0:T(8,128)}, bf16[8,2,16,512]{3,2,1,0:T(8,128)(2,1)}, f32[256,256]{1,0:T(8,128)}, bf16[8,128,512]{2,1,0:T(8,128)(2,1)}, bf16[16,128,512]{2,1,0:T(8,128)(2,1)}) custom-call(bf16[128,512]{1,0:T(8,128)(2,1)} %pad_maximum_fusion.own_ref, bf16[4000,256]{1,0:T(8,128)(2,1)} %bitcast.7, bf16[4000,256]{1,0:T(8,128)(2,1)} %bitcast.9), custom_call_target="tpu_custom_call" | custom-call | tf_op jit(solution)/shard_map/head/pallas_call | solution.py:397
  69.3 90.5 %middle.1 = (s32[2,2048,128]{2,1,0:T(8,128)}, f32[1024,256]{1,0:T(8,128)}, f32[1024,2048]{1,0:T(8,128)}) custom-call(bf16[2,80,128]{2,1,0:T(8,128)(2,1)} %constant.62.clone.h_ref, bf16[80,240]{1,0:T(8,128)(2,1)} %constant.63.clone.hx_ref, bf16[80,240]{1,0:T(8,128)(2,1)} %constant.64.clone.hxt_ref, bf16[80,240]{1,0:T(8,128)(2,1)} %constant.65.clone.hy_ref, ...), custom_call_target="tpu_custom_call" | custom-call | tf_op jit(solution)/shard_map/middle/pallas_call | solution.py:707
  159.8 0.0 copy-start
  159.8 1.6 copy-done
  161.4 4.7 %decode.1 = f32[4000,256]{1,0:T(8,128)} custom-call(s32[2,2048,128]{2,1,0:T(8,128)S(1)} %copy-done), custom_call_target="tpu_custom_call" | custom-call | tf_op jit(solution)/shard_map/decode/pallas_call | solution.py:778
  166.1 0.0 copy-start.1
  166.1 8.0 %copy.12 = f32[1024,2048]{1,0:T(8,128)} copy(f32[1024,2048]{1,0:T(8,128)} %get-tuple-element.27) | data formatting | bytes 16777216
  174.1 0.0 copy-done.1
  174.1 1.0 copy.13
  (1 shorter events, 0.0 us)
Async XLA Ops:
  159.8 1.6 copy-start
  166.1 8.0 %copy-start.1 = (f32[1024,256]{1,0:T(8,128)S(1)}, f32[1024,256]{1,0:T(8,128)}, u32[]{:S(2)}) copy-start(f32[1024,256]{1,0:T(8,128)} %get-tuple-element.28) | copy-start | bytes 3145732

commit v3 on v2

--- a/solution.py
+++ b/solution.py
@@ -108,7 +108,7 @@
     return both[:, :PB], both[:, PB:]
 
 
-def invert_factor(pa, pb, inv_ref, w):
+def invert_factor(pa, pb, inv_ref, w, after):
     i0 = lax.broadcasted_iota(jnp.int32, (PB, PB), 0)
     i1 = lax.broadcasted_iota(jnp.int32, (PB, PB), 1)
     eye = (i0 == i1).astype(f32)
@@ -141,6 +141,8 @@
                 row_k = jnp.concatenate([sub == k] * 4, axis=1)
                 panel = jnp.where(row_k, scaled, panel - wide * scaled)
         w[g : g + nb, :] = panel
+        if block in after:
+            after[block]()
         if g + nb < PB:
             left = panel[:, g + nb : PB] if (g + nb) % 128 == 0 else panel[:, :PB]
             if (g + nb) % 128 == 0:
@@ -187,7 +189,7 @@
     own_ref, phi_ref, psi_ref,
     out_ref, pivot_ref, inv_ref, rows_ref, cols_ref,
     phi, psi, w, work, peak, send1, recv1, send2, recv2, send3, recv3,
-    send_row, recv_row, send_move, recv_move, send_col, recv_col, send_core, recv_core, local,
+    send_row, recv_row, send_move, recv_move, send_col, recv_col, local,
 ):
     r = lax.axis_index("row")
     c = lax.axis_index("col")
@@ -234,6 +236,50 @@
     def _():
         pl.semaphore_wait(barrier, COLS + ROWS - 2)
 
+    x = r // 4
+    zl = lax.rem(half, 2)
+    y = c // 2
+    zh = lax.rem(c, 2)
+    mate_col = y * 2 + 1 - zh
+    mate_half = x * 2 + 1 - zl
+    mate_row = mate_half * 2 + core
+
+    keep_rows = pltpu.make_async_copy(own_ref, rows_ref.at[c], local.at[3])
+    goal_half = goal_row // 2
+    keep_move = pltpu.make_async_copy(own_ref, cols_ref.at[goal_half], local.at[4])
+    move = remote(own_ref, cols_ref.at[goal_half], send_move, recv_move, at(goal_row, goal_col))
+
+    def rows_mate(block):
+        return remote(
+            own_ref, rows_ref.at[block], send_row.at[0], recv_row.at[0], at(r, mate_col)
+        )
+
+    def rows_pair(pair, d, device):
+        blocks = rows_ref.at[pl.ds(pair * 2, 2)]
+        return remote(blocks, blocks, send_row.at[d], recv_row.at[d], at(r, device * 2 + zh))
+
+    def cols_block(block, send, recv, row):
+        return remote(cols_ref.at[block], cols_ref.at[block], send, recv, at(row, c))
+
+    def ahead(v, d):
+        return lax.rem(v + d, 4)
+
+    def cols_x(v, d, i, row):
+        n = 1 + 2 * (d - 1) + i
+        block = v * 2 + (zl if i == 0 else 1 - zl)
+        return cols_block(block, send_col.at[n], recv_col.at[n], row)
+
+    keep_rows.start()
+    rows_mate(c).start()
+
+    @pl.when(jnp.logical_not(stays))
+    def _():
+        move.start()
+
+    @pl.when(stays)
+    def _():
+        keep_move.start()
+
     def scatter(owner, j):
         return remote(
             own_ref.at[pl.ds(pl.multiple_of(j * 16, 16), 16)],
@@ -284,88 +330,44 @@
             pivot_ref.at[source], pivot_ref.at[source], send3.at[d], recv3.at[d], at(r, source)
         ).wait_recv()
 
-    keep_rows = pltpu.make_async_copy(own_ref, rows_ref.at[c], local.at[3])
-    keep_rows.start()
-    move = remote(own_ref, cols_ref.at[goal_row], send_move, recv_move, at(goal_row, goal_col))
-    keep_move = pltpu.make_async_copy(own_ref, cols_ref.at[goal_row], local.at[4])
-
-    @pl.when(jnp.logical_not(stays))
-    def _():
-        move.start()
-
-    @pl.when(stays)
-    def _():
-        keep_move.start()
-
-    def row_send(d):
-        return remote(
-            own_ref, rows_ref.at[c], send_row.at[d], recv_row.at[d], at(r, lax.rem(c + d, COLS))
-        )
-
-    for d in range(1, COLS):
-        row_send(d).start()
-
+    def step_mates():
+        keep_rows.wait()
+        rows_mate(mate_col).wait_recv()
+        for d in range(1, 4):
+            rows_pair(y, d, ahead(y, d)).start()
+
+        @pl.when(jnp.logical_not(stays))
+        def _():
+            remote(
+                own_ref, cols_ref.at[half], send_move, recv_move, at(source_row, source_col)
+            ).wait_recv()
+
+        @pl.when(stays)
+        def _():
+            keep_move.wait()
+
+        cols_block(half, send_col.at[0], recv_col.at[0], mate_row).start()
+
+    def step_x():
+        cols_block(mate_half, send_col.at[0], recv_col.at[0], mate_row).wait_recv()
+        for i in range(2):
+            for d in range(1, 4):
+                cols_x(x, d, i, ahead(x, d) * 4 + zl * 2 + core).start()
+
+    step_mates()
     pa, pb = pivot_halves(pivot_ref)
-    invert_factor(pa, pb, inv_ref, w)
-
-    @pl.when(jnp.logical_not(stays))
-    def _():
-        remote(
-            own_ref, cols_ref.at[r], send_move, recv_move, at(source_row, source_col)
-        ).wait_recv()
-
-    @pl.when(stays)
-    def _():
-        keep_move.wait()
-
-    def col_send(d):
-        return remote(
-            cols_ref.at[r],
-            cols_ref.at[r],
-            send_col.at[d],
-            recv_col.at[d],
-            at(lax.rem(half + d, COLS) * 2 + core, c),
-        )
-
-    for d in range(1, COLS):
-        col_send(d).start()
-
-    def core_send(d):
-        block = lax.rem(half + COLS - d, COLS) * 2 + core
-        return remote(
-            cols_ref.at[block],
-            cols_ref.at[block],
-            send_core.at[d],
-            recv_core.at[d],
-            at(half * 2 + 1 - core, c),
-        )
-
-    core_send(0).start()
+    invert_factor(pa, pb, inv_ref, w, {2: step_x})
     for load in loads:
         load.wait()
     fit(pa, pb, inv_ref[...], phi, psi, out_ref, work, peak)
 
-    for d in range(1, COLS):
-        block = lax.rem(half + COLS - d, COLS) * 2 + core
-        remote(
-            cols_ref.at[block], cols_ref.at[block], send_col.at[d], recv_col.at[d], at(block, c)
-        ).wait_recv()
-        core_send(d).start()
-    keep_rows.wait()
-    for d in range(1, COLS):
-        source = lax.rem(c + COLS - d, COLS)
-        remote(
-            own_ref, rows_ref.at[source], send_row.at[d], recv_row.at[d], at(r, source)
-        ).wait_recv()
-    for d in range(COLS):
-        block = lax.rem(half + COLS - d, COLS) * 2 + 1 - core
-        remote(
-            cols_ref.at[block],
-            cols_ref.at[block],
-            send_core.at[d],
-            recv_core.at[d],
-            at(half * 2 + 1 - core, c),
-        ).wait_recv()
+    for d in range(1, 4):
+        source = ahead(y, 4 - d)
+        rows_pair(source, d, source).wait_recv()
+    for d in range(1, 4):
+        source = ahead(x, 4 - d)
+        for i in range(2):
+            cols_x(source, d, i, source * 4 + zl * 2 + core).wait_recv()
 
     @pl.when(jnp.logical_not(stays))
     def _():
@@ -373,10 +375,12 @@
 
     for d in range(1, COLS):
         across(d).wait_send()
-        row_send(d).wait_send()
-        col_send(d).wait_send()
-    for d in range(COLS):
-        core_send(d).wait_send()
+    rows_mate(c).wait_send()
+    cols_block(half, send_col.at[0], recv_col.at[0], mate_row).wait_send()
+    for d in range(1, 4):
+        rows_pair(y, d, ahead(y, d)).wait_send()
+        for i in range(2):
+            cols_x(x, d, i, ahead(x, d) * 4 + zl * 2 + core).wait_send()
 
     @pl.when(r == 0)
     def _():
@@ -393,7 +397,7 @@
 
 def head(own, phi, psi):
     dma = pltpu.SemaphoreType.DMA
-    anywhere = pl.BlockSpec(memory_space=pl.ANY)
+    anywhere = pl.BlockSpec(memory_space=pltpu.HBM)
     return pl.pallas_call(
         head_kernel,
         out_shape=(
@@ -401,7 +405,7 @@
             jax.ShapeDtypeStruct((COLS, 2, 16, 2 * PB), bf16),
             jax.ShapeDtypeStruct((PB, PB), f32),
             jax.ShapeDtypeStruct((COLS, 128, 2 * PB), bf16),
-            jax.ShapeDtypeStruct((ROWS, 128, 2 * PB), bf16),
+            jax.ShapeDtypeStruct((COLS, 128, 2 * PB), bf16),
         ),
         in_specs=[VMEM, anywhere, anywhere],
         out_specs=(VMEM,) * 5,
@@ -423,18 +427,33 @@
             dma,
             dma((COLS,)),
             dma((COLS,)),
-            dma((COLS,)),
-            dma((COLS,)),
             dma((5,)),
         ],
         compiler_params=pltpu.CompilerParams(
-            collective_id=1, has_side_effects=True, vmem_limit_bytes=60 << 20
+            collective_id=1, has_side_effects=True, vmem_limit_bytes=36 << 20
         ),
         name="head",
     )(own, phi, psi)
 
 
-def half_convolution(f, hx, hxt, hy, wz, wzt, got, sent, high, low, planes, lines, flat, peak):
+def fill_factors(factors):
+    def signed(index):
+        return jnp.where(2 * index < N, index, index - N).astype(f32)
+
+    ky = signed(lax.broadcasted_iota(jnp.int32, (N, 128), 0))
+    kz = signed(lax.broadcasted_iota(jnp.int32, (N, 128), 1))
+    base = ky * ky + kz * kz
+
+    @pl.loop(0, N)
+    def _(kx):
+        fx = signed(jnp.full((N, 128), kx, jnp.int32))
+        squared = base + fx * fx
+        factor = (4.0 / math.pi / (N * N * N)) / jnp.maximum(squared, 1.0)
+        at = pl.ds(pl.multiple_of(kx * N, 16), N)
+        factors[at, :] = jnp.where(squared > 0.5, factor, 0.0)
+
+
+def half_convolution(hx, hxt, hy, wz, wzt, factors, got, sent, high, low, planes, lines, flat, peak):
     scale = load_scale(got)
 
     @pl.loop(0, 4)
@@ -483,27 +502,15 @@
             for s in range(2):
                 lines[line_at((pair * 2 + s) * 5 + yy), :] = out[s]
 
-    def signed(index):
-        return jnp.where(2 * index < N, index, index - N).astype(f32)
-
-    ky = signed(lax.broadcasted_iota(jnp.int32, (N, 128), 0))
-    kz = signed(lax.broadcasted_iota(jnp.int32, (N, 128), 1))
-    base = ky * ky + kz * kz
-
     @pl.loop(0, N // 8)
     def _(group):
         ats = [pl.ds(group * 8 + t, N, stride=N) for t in range(8)]
         datas = [lines[at, :] for at in ats]
         outs = []
         for t in range(0, 8, 2):
-            factors = []
-            for s in range(2):
-                fx = signed(jnp.full((N, 128), group * 8 + t + s, jnp.int32))
-                squared = base + fx * fx
-                factor = (4.0 / math.pi / (N * N * N)) / jnp.maximum(squared, 1.0)
-                factors.append(jnp.where(squared > 0.5, factor, 0.0))
+            factor = [factors[line_at(group * 8 + t + s), :] for s in range(2)]
             out = mm3(hy, jnp.concatenate(datas[t : t + 2], axis=1))
-            outs.extend(both(mm3(hy, out * jnp.concatenate(factors, axis=1))))
+            outs.extend(both(mm3(hy, out * jnp.concatenate(factor, axis=1))))
         for at, out in zip(ats, outs, strict=True):
             lines[at, :] = out
 
@@ -553,15 +560,16 @@
     return mm_nt(left[:, :PB], right[:, :PB]) * mm_nt(left[:, PB:], right[:, PB:])
 
 
-def schur_tiles(pivot_ref, inv_ref, rows_ref, cols_ref, schur_ref, panel_ref, left3, right3, tiles, out_sem, r, c):
+def shifted(gram, row, column):
+    i = row + lax.broadcasted_iota(jnp.int32, gram.shape, 0)
+    j = column + lax.broadcasted_iota(jnp.int32, gram.shape, 1)
+    return gram + jnp.where(i == j, shift_value, 0.0)
+
+
+def panels(pivot_ref, inv_ref, rows_ref, cols_ref, panel_ref, left3, right3, r, c):
     pa, pb = pivot_halves(pivot_ref)
     pivots = jnp.concatenate([pa, pb], axis=1)
     inv = inv_ref[...]
-
-    def shifted(gram, row, column):
-        i = row + lax.broadcasted_iota(jnp.int32, gram.shape, 0)
-        j = column + lax.broadcasted_iota(jnp.int32, gram.shape, 1)
-        return gram + jnp.where(i == j, shift_value, 0.0)
 
     def panel_of(samples, row):
         return lax.dot_general(
@@ -580,9 +588,11 @@
     @pl.loop(0, 8)
     def _(i):
         at = pl.ds(pl.multiple_of(i * 256, 256), 256)
-        high, low = split(panel_of(cols_ref[at, :], c * 2048 + i * 256))
+        high, low = split(panel_of(cols_ref[i].reshape(256, 2 * PB), c * 2048 + i * 256))
         right3[at, :] = jnp.concatenate([high, high, low], axis=1)
 
+
+def schur_tiles(rows_ref, cols_ref, schur_ref, left3, right3, tiles, out_sem, r, c):
     def put(i, slot):
         return pltpu.make_async_copy(
             tiles.at[slot], schur_ref.at[pl.ds(pl.multiple_of(i * 128, 128), 128)], out_sem.at[slot]
@@ -602,9 +612,8 @@
             left = left3[at, :]
             for j in range(4):
                 cols = slice(j * 512, j * 512 + 512)
-                gram = shifted(
-                    grams(rows, cols_ref[cols, :]), r * 1024 + i * 128, c * 2048 + j * 512
-                )
+                samples = cols_ref[2 * j : 2 * j + 2].reshape(512, 2 * PB)
+                gram = shifted(grams(rows, samples), r * 1024 + i * 128, c * 2048 + j * 512)
                 tiles[slot, :, cols] = gram - mm_nt(left, right3[cols, :])
             put(i, slot).start()
 
@@ -615,8 +624,8 @@
 def middle_kernel(
     h_ref, hx_ref, hxt_ref, hy_ref, codes_ref, pivot_ref, inv_ref, rows_ref, cols_ref,
     back_ref, panel_ref, schur_ref,
-    got, sent, wz, wzt, high, low, planes, lines, flat, peak, left3, right3, tiles,
-    send_there, recv_there, send_back, recv_back, own_sem, out_sem,
+    got, sent, wz, wzt, high, low, planes, lines, flat, peak, left3, right3, tiles, samples, factors,
+    send_there, recv_there, send_back, recv_back, own_sem, out_sem, twin_sem,
 ):
     r = lax.axis_index("row")
     c = lax.axis_index("col")
@@ -659,8 +668,23 @@
     def wait_own(source, target, keep):
         pltpu.make_async_copy(source.at[block(me)], target.at[block(me)], keep).wait()
 
+    core = lax.rem(r, 2)
+    keep_samples = pltpu.make_async_copy(cols_ref, samples.at[:, core], twin_sem.at[0])
+
+    def twin_copy(k):
+        return pltpu.make_async_remote_copy(
+            cols_ref,
+            samples.at[:, k],
+            twin_sem.at[1],
+            twin_sem.at[2],
+            device_id={"row": r + 1 - 2 * core, "col": c},
+            device_id_type=MESH,
+        )
+
     for f in range(2):
         send_all(codes_ref.at[f], got.at[f], send_there.at[f], recv_there.at[f], own_sem.at[f])
+    keep_samples.start()
+    twin_copy(core).start()
 
     wz[...] = jnp.zeros_like(wz)
     wzt[...] = jnp.zeros_like(wzt)
@@ -673,23 +697,26 @@
                 lane = part * 256 + 128 * s
                 wzt[n, first : first + 80, lane : lane + 128] = h
 
-    schur_tiles(
-        pivot_ref, inv_ref, rows_ref, cols_ref, schur_ref, panel_ref, left3, right3, tiles, out_sem, r, c
-    )
+    fill_factors(factors)
+    keep_samples.wait()
+    twin_copy(1 - core).wait_recv()
+    panels(pivot_ref, inv_ref, rows_ref, samples, panel_ref, left3, right3, r, c)
     matrices = (hx_ref[...], hxt_ref[...], hy_ref[...])
     for f in range(2):
         wait_own(codes_ref.at[f], got.at[f], own_sem.at[f])
         wait_all(got.at[f], recv_there.at[f])
         half_convolution(
-            f, *matrices, wz, wzt, got.at[f], sent.at[f], high, low, planes, lines, flat, peak
+            *matrices, wz, wzt, factors, got.at[f], sent.at[f], high, low, planes, lines, flat, peak
         )
         send_all(sent.at[f], back_ref.at[f], send_back.at[f], recv_back.at[f], own_sem.at[2 + f])
+    schur_tiles(rows_ref, samples, schur_ref, left3, right3, tiles, out_sem, r, c)
     for f in range(2):
         wait_own(sent.at[f], back_ref.at[f], own_sem.at[2 + f])
         wait_all(back_ref.at[f], recv_back.at[f])
     for f in range(2):
         wait_all(codes_ref.at[f], send_there.at[f])
         wait_all(sent.at[f], send_back.at[f])
+    twin_copy(core).wait_send()
 
 
 def side_by_side(a):
@@ -727,15 +754,18 @@
             pltpu.VMEM((NMU // ROWS, 768), bf16),
             pltpu.VMEM((NMU // COLS, 768), bf16),
             pltpu.VMEM((2, 128, NMU // COLS), f32),
+            pltpu.VMEM((COLS, 2, 128, 2 * PB), bf16),
+            pltpu.VMEM((N * N, 128), f32),
             dma((2,)),
             dma((2,)),
             dma((2,)),
             dma((2,)),
             dma((4,)),
             dma((2,)),
+            dma((3,)),
         ],
         compiler_params=pltpu.CompilerParams(
-            collective_id=2, has_side_effects=True, vmem_limit_bytes=60 << 20
+            collective_id=2, has_side_effects=True, vmem_limit_bytes=44 << 20
         ),
         name="middle",
     )(
@@ -751,7 +781,22 @@
     )
 
 
-def decode_kernel(in_ref, out_ref):
+def decode_kernel(in_ref, schur_ref, panel_ref, out_ref, schur_out, panel_out, held, sems):
+    def pieces(source, target, which):
+        copies = []
+        for i in range(8):
+            at = pl.ds(i * 128, 128)
+            ends = [ref if ref is held else ref.at[at] for ref in (source, target)]
+            ends = [ref.at[i] if ref is held else ref for ref in ends]
+            copies.append(pltpu.make_async_copy(*ends, sems.at[which, i]))
+        return copies
+
+    loads = pieces(schur_ref, held, 0)
+    stores = pieces(held, schur_out, 1)
+    panel_store = pltpu.make_async_copy(panel_ref, panel_out, sems.at[2, 0])
+    panel_store.start()
+    for load in loads:
+        load.start()
     for f in range(2):
         words_ref = in_ref.at[f]
         scale = load_scale(words_ref)
@@ -772,17 +817,37 @@
         words = words_ref[pl.ds(15, 128, stride=16), :]
         put(15, low_of(words))
         out_ref[3968:4000, lanes] = (high_of(words) * scale).T[:32]
-
-
-def decode(codes):
+        if f == 0:
+            for load, store in zip(loads, stores, strict=True):
+                load.wait()
+                store.start()
+    for store in stores:
+        store.wait()
+    panel_store.wait()
+
+
+def decode(codes, schur, panel):
+    anywhere = pl.BlockSpec(memory_space=pltpu.HBM)
     return pl.pallas_call(
         decode_kernel,
-        out_shape=jax.ShapeDtypeStruct((CELLS, PB), f32),
-        in_specs=[VMEM],
-        out_specs=VMEM,
-        compiler_params=pltpu.CompilerParams(vmem_limit_bytes=20 << 20),
+        out_shape=(
+            jax.ShapeDtypeStruct((CELLS, PB), f32),
+            jax.ShapeDtypeStruct(schur.shape, f32),
+            jax.ShapeDtypeStruct(panel.shape, f32),
+        ),
+        in_specs=[VMEM, anywhere, VMEM],
+        out_specs=(VMEM, anywhere, anywhere),
+        scratch_shapes=[
+            pltpu.VMEM((8, 128, NMU // COLS), f32),
+            pltpu.SemaphoreType.DMA((3, 8)),
+        ],
+        compiler_params=pltpu.CompilerParams(vmem_limit_bytes=24 << 20),
         name="decode",
-    )(codes)
+    )(codes, schur, panel)
+
+
+def in_hbm(a):
+    return pltpu.with_memory_space_constraint(a, pltpu.HBM)
 
 
 def on_device(phi, psi, points):
@@ -800,11 +865,11 @@
     own = jnp.concatenate(
         [jnp.take(flat_phi, local_cell, axis=0), jnp.take(flat_psi, local_cell, axis=0)], axis=1
     )
-    codes, pivots, inverse, row_samples, col_samples = head(own, flat_phi, flat_psi)
+    codes, pivots, inverse, row_samples, col_samples = head(own, in_hbm(flat_phi), in_hbm(flat_psi))
     row_samples = row_samples.reshape(NMU // ROWS, 2 * PB)
-    col_samples = col_samples.reshape(NMU // COLS, 2 * PB)
     back, panel, schur = middle(codes, pivots, inverse, row_samples, col_samples)
-    potential = decode(back).reshape(plane_count, line_count, depth_count, PB)
+    potential, schur, panel = decode(back, in_hbm(schur), panel)
+    potential = potential.reshape(plane_count, line_count, depth_count, PB)
     return (schur, panel, potential)
 
 

time: 175 us -> 156 us (0.89); the launches traced: 175 us -> 154 us
  local copies, waits for them, and re-layouts: 15.7 us -> 5.22 us
  Pallas kernels: 157 us -> 147 us
    pallas_call x1, Pallas kernels: 62 us -> 50 us  [head(): pl.pallas_call(head_kernel, out_shape=(jax.ShapeDtypeStruct((2, WORDS, 12...]
    unnamed x6 -> x8, local copies, waits for them, and re-layouts: 10.5 us -> 0.03 us
    pallas_call x1, Pallas kernels: 4.69 us -> 9.22 us  [decode(): pl.pallas_call(decode_kernel, out_shape=(jax.ShapeDtypeStruct((CELLS, PB)...]
    pallas_call x1, Pallas kernels: 90.5 us -> 87.5 us  [middle(): pl.pallas_call(middle_kernel, out_shape=(jax.ShapeDtypeStruct((2, WORDS,...]
where the time goes in v3:
time: 156 us; the launch traced here: 154 us
  Pallas kernels  147 us (94%)
  local copies, waits for them, and re-layouts  5.22 us (3%)
    pallas_call x1, Pallas kernels, middle(): pl.pallas_call(middle_kernel, out_shape=(jax.ShapeDtypeStruct((2, WORDS,...  87.5 us
    pallas_call x1, Pallas kernels, head(): pl.pallas_call(head_kernel, out_shape=(jax.ShapeDtypeStruct((2, WORDS, 12...  50 us
    pallas_call x1, Pallas kernels, decode(): pl.pallas_call(decode_kernel, out_shape=(jax.ShapeDtypeStruct((CELLS, PB)...  9.22 us

profile of v3, /device:TPU:1, one launch (start us, length us, event | category | flops | bytes accessed | tf_op | source)
XLA Modules:
  0.0 153.6 jit_solution(8548576578449731039)
XLA Ops:
  0.6 0.7 compare_and_fusion
  1.3 2.6 %gather_fusion.1 = bf16[128,256]{1,0:T(8,128)(2,1)S(1)} fusion(bf16[4000,256]{1,0:T(8,128)(2,1)} %bitcast.7, s32[1024]{0:T(1024)S(1)} %pad_clamp_fusion), kind=kCustom, calls=%fused_computation.1.clone | custom fusion | bytes 131584 | tf_op jit(solution)/shard_map/jit(_take)/gather | solution.py:866
  3.9 2.6 %gather_fusion = bf16[128,256]{1,0:T(8,128)(2,1)S(1)} fusion(bf16[4000,256]{1,0:T(8,128)(2,1)} %bitcast.5, s32[1024]{0:T(1024)S(1)} %pad_clamp_fusion), kind=kCustom, calls=%fused_computation.clone | custom fusion | bytes 131584 | tf_op jit(solution)/shard_map/jit(_take)/gather | solution.py:866
  6.5 0.1 broadcast_select_fusion.1
  6.6 0.0 copy-start
  6.7 0.0 copy-start.1
  6.7 0.0 copy-start.2
  6.7 0.0 copy-start.3
  6.7 50.0 %head.1 = (s32[2,2048,128]{2,1,0:T(8,128)S(1)}, bf16[8,2,16,512]{3,2,1,0:T(8,128)(2,1)S(1)}, f32[256,256]{1,0:T(8,128)S(1)}, bf16[8,128,512]{2,1,0:T(8,128)(2,1)S(1)}, bf16[8,128,512]{2,1,0:T(8,128)(2,1)S(1)}) custom-call(bf16[128,512]{1,0:T(8,128)(2,1)S(1)} %pad_maximum_fusion.own_ref, bf16[4000,256]{1,0:T(8,128)(2,1)} %bitcast.6, bf16[4000,256]{1,0:T(8,128)(2,1)} %bitcast.8), custom_call_target="tpu_custom_call" | custom-call | tf_op jit(solution)/shard_map/head/pallas_call | solution.py:401
  56.7 0.0 copy-done
  56.7 0.0 copy-done.1
  56.7 0.0 copy-done.2
  56.7 0.0 copy-done.3
  56.7 87.5 %middle.1 = (s32[2,2048,128]{2,1,0:T(8,128)S(1)}, f32[1024,256]{1,0:T(8,128)S(1)}, f32[1024,2048]{1,0:T(8,128)}) custom-call(bf16[2,80,128]{2,1,0:T(8,128)(2,1)S(1)} %copy-done.3, bf16[80,240]{1,0:T(8,128)(2,1)S(1)} %copy-done.2, bf16[80,240]{1,0:T(8,128)(2,1)S(1)} %copy-done.1, bf16[80,240]{1,0:T(8,128)(2,1)S(1)} %copy-done, ...), custom_call_target="tpu_custom_call" | custom-call | tf_op jit(solution)/shard_map/middle/pallas_call | solution.py:734
  144.2 9.2 %decode.1 = (f32[4000,256]{1,0:T(8,128)}, f32[1024,2048]{1,0:T(8,128)}, f32[1024,256]{1,0:T(8,128)}) custom-call(s32[2,2048,128]{2,1,0:T(8,128)S(1)} %get-tuple-element.20.in_ref, f32[1024,2048]{1,0:T(8,128)} %get-tuple-element.21.schur_ref, f32[1024,256]{1,0:T(8,128)S(1)} %get-tuple-element.22.panel_ref), custom_call_target="tpu_custom_call" | custom-call | tf_op jit(solution)/shard_map/decode/pallas_call | solution.py:831
  (2 shorter events, 0.0 us)
Async XLA Ops:
  6.6 50.0 %copy-start = (bf16[80,240]{1,0:T(8,128)(2,1)S(1)}, bf16[80,240]{1,0:T(8,128)(2,1)}, u32[]{:S(2)}) copy-start(bf16[80,240]{1,0:T(8,128)(2,1)} %constant.65.clone.hy_ref) | copy-start | bytes 115204
  6.7 50.0 %copy-start.1 = (bf16[80,240]{1,0:T(8,128)(2,1)S(1)}, bf16[80,240]{1,0:T(8,128)(2,1)}, u32[]{:S(2)}) copy-start(bf16[80,240]{1,0:T(8,128)(2,1)} %constant.64.clone.hxt_ref) | copy-start | bytes 115204
  6.7 50.0 %copy-start.2 = (bf16[80,240]{1,0:T(8,128)(2,1)S(1)}, bf16[80,240]{1,0:T(8,128)(2,1)}, u32[]{:S(2)}) copy-start(bf16[80,240]{1,0:T(8,128)(2,1)} %constant.63.clone.hx_ref) | copy-start | bytes 115204
  6.7 50.0 %copy-start.3 = (bf16[2,80,128]{2,1,0:T(8,128)(2,1)S(1)}, bf16[2,80,128]{2,1,0:T(8,128)(2,1)}, u32[]{:S(2)}) copy-start(bf16[2,80,128]{2,1,0:T(8,128)(2,1)} %constant.62.clone.h_ref) | copy-start | bytes 122884

commit v4 on v3

--- a/solution.py
+++ b/solution.py
@@ -1,5 +1,5 @@
-import functools
 import math
+import random
 
 import jax
 import jax.numpy as jnp
@@ -27,6 +27,13 @@
 VMEM = pl.BlockSpec(memory_space=pltpu.VMEM)
 f32 = jnp.float32
 bf16 = jnp.bfloat16
+
+
+def far_first():
+    every = [(a, b, c, k) for a in range(4) for b in range(4) for c in range(4) for k in range(2)]
+    every.remove((0, 0, 0, 0))
+    random.Random(1).shuffle(every)
+    return sorted(every, key=lambda d: -sum(min(v, 4 - v) for v in d[:3]))
 
 
 def hartley():
@@ -646,18 +653,26 @@
 
     pl.semaphore_wait(barrier, DEVICES - 1)
 
+    x, z, y = r // 4, lax.rem(c, 2) * 2 + lax.rem(r // 2, 2), c // 2
+    xs = [lax.rem(x + d, 4) * 4 for d in range(4)]
+    ys = [lax.rem(y + d, 4) * 2 for d in range(4)]
+    zs = [lax.rem(z + d, 4) for d in range(4)]
+    z_rows = [lax.rem(v, 2) * 2 for v in zs]
+    z_cols = [v // 2 for v in zs]
+    ks = [lax.rem(r + d, 2) for d in range(2)]
+    z_cores = [[v + k for k in ks] for v in z_rows]
+    cols = [[v + w for w in z_cols] for v in ys]
+
     def send_all(source, target, send, recv, keep):
         pltpu.make_async_copy(source.at[block(me)], target.at[block(me)], keep).start()
-
-        @pl.loop(1, DEVICES)
-        def _(i):
-            device, where = at(i)
+        for dx, dy, dz, dk in far_first():
+            row, col = xs[dx] + z_cores[dz][dk], cols[dy][dz]
             pltpu.make_async_remote_copy(
-                source.at[block(device)],
+                source.at[block(row * COLS + col)],
                 target.at[block(me)],
                 send,
                 recv,
-                device_id=where,
+                device_id={"row": row, "col": col},
                 device_id_type=MESH,
             ).start()
 
@@ -781,7 +796,9 @@
     )
 
 
-def decode_kernel(in_ref, schur_ref, panel_ref, out_ref, schur_out, panel_out, held, sems):
+def decode_kernel(
+    in_ref, schur_ref, panel_ref, result_ref, schur_out, panel_out, held, out_ref, sems, out_sems
+):
     def pieces(source, target, which):
         copies = []
         for i in range(8):
@@ -797,32 +814,42 @@
     panel_store.start()
     for load in loads:
         load.start()
-    for f in range(2):
-        words_ref = in_ref.at[f]
-        scale = load_scale(words_ref)
-        lanes = slice(f * 128, f * 128 + 128)
-
-        def put(tile, value):
-            block = (value * scale).T
-            at = pl.ds(pl.multiple_of(tile * 128, 128), 128)
-            out_ref[at, lanes] = block
-
-        @pl.loop(0, 5)
-        def _(group):
-            for t in range(3):
-                words = words_ref[pl.ds(group * 3 + t, 128, stride=16), :]
-                put(group * 3 + t, low_of(words))
-                put(group * 3 + t + 16, high_of(words))
-
-        words = words_ref[pl.ds(15, 128, stride=16), :]
-        put(15, low_of(words))
-        out_ref[3968:4000, lanes] = (high_of(words) * scale).T[:32]
-        if f == 0:
-            for load, store in zip(loads, stores, strict=True):
-                load.wait()
-                store.start()
+    scales = [load_scale(in_ref.at[f]) for f in range(2)]
+    results = []
+
+    def decoded(j):
+        for f in range(2):
+            lanes = slice(f * 128, f * 128 + 128)
+            words = in_ref[f, pl.ds(j, 128, stride=16), :]
+            out_ref[j * 128 : j * 128 + 128, lanes] = (low_of(words) * scales[f]).T
+            start = (j + 16) * 128
+            rows = min(CELLS - start, 128)
+            out_ref[start : start + rows, lanes] = (high_of(words) * scales[f]).T[:rows]
+
+    def put(start, rows):
+        at = pl.ds(start, rows)
+        copy = pltpu.make_async_copy(
+            out_ref.at[at], result_ref.at[at], out_sems.at[len(results)]
+        )
+        copy.start()
+        results.append(copy)
+
+    for group in range(5):
+        for t in range(3):
+            decoded(group * 3 + t)
+        put(group * 384, 384)
+        put(2048 + group * 384, 384)
+        if group:
+            for piece in (group * 2 - 2, group * 2 - 1):
+                loads[piece].wait()
+                stores[piece].start()
+    decoded(15)
+    put(1920, 128)
+    put(3968, 32)
     for store in stores:
         store.wait()
+    for copy in results:
+        copy.wait()
     panel_store.wait()
 
 
@@ -836,10 +863,12 @@
             jax.ShapeDtypeStruct(panel.shape, f32),
         ),
         in_specs=[VMEM, anywhere, VMEM],
-        out_specs=(VMEM, anywhere, anywhere),
+        out_specs=(anywhere,) * 3,
         scratch_shapes=[
             pltpu.VMEM((8, 128, NMU // COLS), f32),
+            pltpu.VMEM((CELLS, PB), f32),
             pltpu.SemaphoreType.DMA((3, 8)),
+            pltpu.SemaphoreType.DMA((12,)),
         ],
         compiler_params=pltpu.CompilerParams(vmem_limit_bytes=24 << 20),
         name="decode",

time: 156 us -> 149 us (0.955)
  Pallas kernels: 147 us -> 141 us
    pallas_call x1, Pallas kernels: 87.5 us -> 83 us  [middle(): pl.pallas_call(middle_kernel, out_shape=(jax.ShapeDtypeStruct((2, WORDS,...]
where the time goes in v4:
time: 149 us; the launch traced here: 148 us
  Pallas kernels  141 us (95%)
  local copies, waits for them, and re-layouts  5.22 us (4%)
    pallas_call x1, Pallas kernels, middle(): pl.pallas_call(middle_kernel, out_shape=(jax.ShapeDtypeStruct((2, WORDS,...  83 us
    pallas_call x1, Pallas kernels, head(): pl.pallas_call(head_kernel, out_shape=(jax.ShapeDtypeStruct((2, WORDS, 12...  50 us
    pallas_call x1, Pallas kernels, decode(): pl.pallas_call(decode_kernel, out_shape=(jax.ShapeDtypeStruct((CELLS, PB)...  8.12 us

profile of v4, /device:TPU:1, one launch (start us, length us, event | category | flops | bytes accessed | tf_op | source)
XLA Modules:
  0.0 148.0 jit_solution(7053925301254792300)
XLA Ops:
  0.6 0.7 compare_and_fusion
  1.3 2.6 %gather_fusion.1 = bf16[128,256]{1,0:T(8,128)(2,1)S(1)} fusion(bf16[4000,256]{1,0:T(8,128)(2,1)} %bitcast.7, s32[1024]{0:T(1024)S(1)} %pad_clamp_fusion), kind=kCustom, calls=%fused_computation.1.clone | custom fusion | bytes 131584 | tf_op jit(solution)/shard_map/jit(_take)/gather | solution.py:895
  3.9 2.6 %gather_fusion = bf16[128,256]{1,0:T(8,128)(2,1)S(1)} fusion(bf16[4000,256]{1,0:T(8,128)(2,1)} %bitcast.5, s32[1024]{0:T(1024)S(1)} %pad_clamp_fusion), kind=kCustom, calls=%fused_computation.clone | custom fusion | bytes 131584 | tf_op jit(solution)/shard_map/jit(_take)/gather | solution.py:895
  6.5 0.1 broadcast_select_fusion.1
  6.6 0.0 copy-start
  6.7 0.0 copy-start.1
  6.7 0.0 copy-start.2
  6.7 0.0 copy-start.3
  6.7 50.0 %head.1 = (s32[2,2048,128]{2,1,0:T(8,128)S(1)}, bf16[8,2,16,512]{3,2,1,0:T(8,128)(2,1)S(1)}, f32[256,256]{1,0:T(8,128)S(1)}, bf16[8,128,512]{2,1,0:T(8,128)(2,1)S(1)}, bf16[8,128,512]{2,1,0:T(8,128)(2,1)S(1)}) custom-call(bf16[128,512]{1,0:T(8,128)(2,1)S(1)} %pad_maximum_fusion.own_ref, bf16[4000,256]{1,0:T(8,128)(2,1)} %bitcast.6, bf16[4000,256]{1,0:T(8,128)(2,1)} %bitcast.8), custom_call_target="tpu_custom_call" | custom-call | tf_op jit(solution)/shard_map/head/pallas_call | solution.py:408
  56.7 0.0 copy-done
  56.7 0.0 copy-done.1
  56.7 0.0 copy-done.2
  56.7 0.0 copy-done.3
  56.7 83.0 %middle.1 = (s32[2,2048,128]{2,1,0:T(8,128)S(1)}, f32[1024,256]{1,0:T(8,128)S(1)}, f32[1024,2048]{1,0:T(8,128)}) custom-call(bf16[2,80,128]{2,1,0:T(8,128)(2,1)S(1)} %copy-done.3, bf16[80,240]{1,0:T(8,128)(2,1)S(1)} %copy-done.2, bf16[80,240]{1,0:T(8,128)(2,1)S(1)} %copy-done.1, bf16[80,240]{1,0:T(8,128)(2,1)S(1)} %copy-done, ...), custom_call_target="tpu_custom_call" | custom-call | tf_op jit(solution)/shard_map/middle/pallas_call | solution.py:749
  139.7 8.1 %decode.1 = (f32[4000,256]{1,0:T(8,128)}, f32[1024,2048]{1,0:T(8,128)}, f32[1024,256]{1,0:T(8,128)}) custom-call(s32[2,2048,128]{2,1,0:T(8,128)S(1)} %get-tuple-element.20.in_ref, f32[1024,2048]{1,0:T(8,128)} %get-tuple-element.21.schur_ref, f32[1024,256]{1,0:T(8,128)S(1)} %get-tuple-element.22.panel_ref), custom_call_target="tpu_custom_call" | custom-call | tf_op jit(solution)/shard_map/decode/pallas_call | solution.py:858
  (2 shorter events, 0.0 us)
Async XLA Ops:
  6.6 50.0 %copy-start = (bf16[80,240]{1,0:T(8,128)(2,1)S(1)}, bf16[80,240]{1,0:T(8,128)(2,1)}, u32[]{:S(2)}) copy-start(bf16[80,240]{1,0:T(8,128)(2,1)} %constant.65.clone.hy_ref) | copy-start | bytes 115204
  6.7 50.0 %copy-start.1 = (bf16[80,240]{1,0:T(8,128)(2,1)S(1)}, bf16[80,240]{1,0:T(8,128)(2,1)}, u32[]{:S(2)}) copy-start(bf16[80,240]{1,0:T(8,128)(2,1)} %constant.64.clone.hxt_ref) | copy-start | bytes 115204
  6.7 50.0 %copy-start.2 = (bf16[80,240]{1,0:T(8,128)(2,1)S(1)}, bf16[80,240]{1,0:T(8,128)(2,1)}, u32[]{:S(2)}) copy-start(bf16[80,240]{1,0:T(8,128)(2,1)} %constant.63.clone.hx_ref) | copy-start | bytes 115204
  6.7 50.0 %copy-start.3 = (bf16[2,80,128]{2,1,0:T(8,128)(2,1)S(1)}, bf16[2,80,128]{2,1,0:T(8,128)(2,1)}, u32[]{:S(2)}) copy-start(bf16[2,80,128]{2,1,0:T(8,128)(2,1)} %constant.62.clone.h_ref) | copy-start | bytes 122884
